TPU v7x, 32 devices: a whole 2x2x4 slice. The times are simulated.
32 devices in a mesh: row: 4 (over x, core), col: 8 (over z, y).
Axes of the slice: x: 2, y: 2, z: 4, core: 2. Of those that a mesh axis runs over, the one named last changes fastest.
Arguments:
- currents: float32 [3, 131072], P(None, ('row', 'col')), may hold values from -6 to 6
- probes: float32 [3, 131072], P(None, ('row', 'col')), may hold values from -6 to 6
- proj_weights: float32 [4, 131072], P(None, ('row', 'col')), may hold values from 0.5 to 2
- interp_weights: float32 [4, 131072], P(None, ('row', 'col')), may hold values from 0.5 to 2
- owner: int32 [131072, 1], P(('row', 'col')), may hold values from 0 to 31; in each aligned block of 4096 rows (0 to 4095, 4096 to 8191, ...) at most 256 rows name the same one
- cell: int32 [131072], P(('row', 'col')), may hold values from 0 to 129023
- near_list: int32 [1024, 4], P(('row', 'col')), may hold values from 0 to 31
- near_matrix: bfloat16 [1024, 4, 128, 128], P(('row', 'col')), may hold values from -0.25 to 0.25
- kernel_hat: float32 [1, 2048, 2048], P(None, ('row', 'col')), as said below
Outputs:
- forward_out: float32 [3, 131072], P(None, ('row', 'col'))
- adjoint_out: float32 [3, 131072], P(None, ('row', 'col'))
Inputs may be any that keep to these rules, and one draw needn't show every extreme that they name: Among the 4096 elements of one device no owner is named more than 256 times; in every draw some device names some owner exactly 256 times. Every entry is positive, and kernel_hat[t, ky, kx] equals kernel_hat[t, (2048 - ky) mod 2048, (2048 - kx) mod 2048].
All inputs are finite; a program needn't handle non-finite values.
Results may differ from a plain program's by a relative error of at most 0.0003.
Values sent between devices are 32-bit elements; how exact they have to be, the bound alone decides.
No kernel may reach another device: no remote copies, remote signals or barrier semaphores. Data moves between devices by JAX's collectives and lax.ppermute only.
A program may use at most 320 MiB of HBM per device.

v0:
```python
import math

import jax
import jax.numpy as jnp
from jax import lax
from jax.sharding import PartitionSpec as P

exact_math = lax.Precision.HIGHEST


def phase_table(row_count, col_count, length, direction):
    row_ids = jnp.arange(row_count, dtype=jnp.int32)
    col_ids = jnp.arange(col_count, dtype=jnp.int32)
    turns = row_ids[:, None] * col_ids[None, :] % length
    angle = turns.astype(jnp.float32) * (2.0 * math.pi / length)
    return (jnp.cos(angle), direction * jnp.sin(angle))


def contract(pattern, real_part, imag_part, cos_table, sin_table):
    real_cos = jnp.einsum(pattern, real_part, cos_table, precision=exact_math)
    real_sin = jnp.einsum(pattern, real_part, sin_table, precision=exact_math)
    if imag_part is None:
        return (real_cos, real_sin)
    imag_cos = jnp.einsum(pattern, imag_part, cos_table, precision=exact_math)
    imag_sin = jnp.einsum(pattern, imag_part, sin_table, precision=exact_math)
    return (real_cos - imag_sin, real_sin + imag_cos)


def rotate(real_part, imag_part, cos_table, sin_table):
    return (
        real_part * cos_table - imag_part * sin_table,
        real_part * sin_table + imag_part * cos_table,
    )


def radix_split(length):
    lower = int(math.isqrt(length))
    while length % lower != 0:
        lower = lower - 1
    return (lower, length // lower)


def on_device(
    currents, probes, proj_weights, interp_weights, owner, cell, near_list, near_matrix, kernel_hat
):
    row_count = lax.axis_size("row")
    col_count = lax.axis_size("col")
    devices = row_count * col_count
    elem_count = currents.shape[1]
    capacity = 2 * elem_count // devices
    dz_count, ky_local, grid_x = kernel_hat.shape
    planes = (dz_count + 1) // 2
    grid_y = ky_local * devices
    x_local = grid_x // devices
    slots = devices * capacity
    target = owner[:, 0]
    owner_ids = jnp.arange(devices, dtype=jnp.int32)
    member = (target[:, None] == owner_ids[None, :]).astype(jnp.int32)
    before = jnp.cumsum(member, axis=0) - member
    slot_index = jnp.sum(before * member, axis=1)
    position = target * capacity + slot_index
    payload = jnp.concatenate([currents, probes, proj_weights, interp_weights], axis=0)
    outgoing = jnp.zeros((14, slots), jnp.float32).at[:, position].set(payload)
    cell_out = jnp.zeros((1, slots), jnp.int32).at[:, position].set(cell[None, :])
    arrived, cell_in = (
        lax.all_to_all(
            outgoing.reshape(14, devices, capacity),
            ("row", "col"),
            split_axis=1,
            concat_axis=1,
            tiled=True,
        ),
        lax.all_to_all(
            cell_out.reshape(1, devices, capacity),
            ("row", "col"),
            split_axis=1,
            concat_axis=1,
            tiled=True,
        ),
    )
    arrived = arrived.reshape(14, slots)
    cell_in = cell_in.reshape(slots)
    plane_of = cell_in // ((x_local - 1) * grid_y)
    row_of = cell_in // grid_y % (x_local - 1)
    col_of = cell_in % grid_y
    cells_list = []
    for shift_x in range(2):
        for shift_y in range(2):
            cells_list.append(
                plane_of * (x_local * grid_y)
                + (row_of + shift_x) * grid_y
                + (col_of + shift_y) % grid_y
            )
    stencil = jnp.stack(cells_list)
    spread_w = arrived[6:10]
    sample_w = arrived[10:14]
    sources = jnp.concatenate(
        [arrived[0:3, None, :] * spread_w[None], arrived[3:6, None, :] * sample_w[None]], axis=0
    )
    cells_total = planes * x_local * grid_y
    grid_vals = (
        jnp.zeros((6, cells_total), jnp.float32)
        .at[:, stencil.reshape(-1)]
        .add(sources.reshape(6, -1))
    )
    grid_vals = grid_vals.reshape(6 * planes, x_local, grid_y)
    kernel_view = kernel_hat.reshape(dz_count, ky_local, x_local, devices)
    kernel_t = jnp.transpose(kernel_view, (0, 3, 1, 2)) * (1.0 / (grid_x * grid_y))
    lower_y, upper_y = radix_split(grid_y)

    def convolve(field_grid):
        stacked = field_grid.shape[0]
        fields = stacked // planes
        digits = field_grid.reshape(stacked, x_local, lower_y, upper_y)
        digits_imag = None
        cos_a, sin_a = phase_table(lower_y, lower_y, lower_y, -1.0)
        real_part, imag_part = contract("mxab,ak->mxkb", digits, digits_imag, cos_a, sin_a)
        twist_cos, twist_sin = phase_table(lower_y, upper_y, grid_y, -1.0)
        real_part, imag_part = rotate(real_part, imag_part, twist_cos, twist_sin)
        cos_b, sin_b = phase_table(upper_y, upper_y, upper_y, -1.0)
        real_part, imag_part = contract("mxkb,bq->qkxm", real_part, imag_part, cos_b, sin_b)
        real_part = real_part.reshape(devices, ky_local, x_local * stacked)
        imag_part = imag_part.reshape(devices, ky_local, x_local * stacked)
        real_part, imag_part = (
            lax.all_to_all(real_part, ("row", "col"), split_axis=0, concat_axis=0, tiled=True),
            lax.all_to_all(imag_part, ("row", "col"), split_axis=0, concat_axis=0, tiled=True),
        )
        real_part = real_part.reshape(devices, ky_local, x_local, stacked)
        imag_part = imag_part.reshape(devices, ky_local, x_local, stacked)
        cos_d, sin_d = phase_table(devices, devices, devices, -1.0)
        real_part, imag_part = contract("djxm,dk->kjxm", real_part, imag_part, cos_d, sin_d)
        twist_cos, twist_sin = phase_table(devices, x_local, grid_x, -1.0)
        real_part, imag_part = rotate(
            real_part, imag_part, twist_cos[:, None, :, None], twist_sin[:, None, :, None]
        )
        cos_x, sin_x = phase_table(x_local, x_local, x_local, -1.0)
        real_part, imag_part = contract("kjxm,xq->kjqm", real_part, imag_part, cos_x, sin_x)
        real_five = real_part.reshape(devices, ky_local, x_local, fields, planes)
        imag_five = imag_part.reshape(devices, ky_local, x_local, fields, planes)
        factor = kernel_t[planes - 1][..., None]
        real_sum = factor * real_five[..., 0]
        imag_sum = factor * imag_five[..., 0]
        real_list = [real_sum]
        imag_list = [imag_sum]
        real_part = jnp.stack(real_list, axis=-1).reshape(devices, ky_local, x_local, stacked)
        imag_part = jnp.stack(imag_list, axis=-1).reshape(devices, ky_local, x_local, stacked)
        cos_x, sin_x = phase_table(x_local, x_local, x_local, 1.0)
        real_part, imag_part = contract("kjqm,qx->kjxm", real_part, imag_part, cos_x, sin_x)
        twist_cos, twist_sin = phase_table(devices, x_local, grid_x, 1.0)
        real_part, imag_part = rotate(
            real_part, imag_part, twist_cos[:, None, :, None], twist_sin[:, None, :, None]
        )
        cos_d, sin_d = phase_table(devices, devices, devices, 1.0)
        real_part, imag_part = contract("kjxm,kd->djxm", real_part, imag_part, cos_d, sin_d)
        real_part = real_part.reshape(devices, ky_local, x_local * stacked)
        imag_part = imag_part.reshape(devices, ky_local, x_local * stacked)
        real_part, imag_part = (
            lax.all_to_all(real_part, ("row", "col"), split_axis=0, concat_axis=0, tiled=True),
            lax.all_to_all(imag_part, ("row", "col"), split_axis=0, concat_axis=0, tiled=True),
        )
        real_part = real_part.reshape(upper_y, lower_y, x_local, stacked)
        imag_part = imag_part.reshape(upper_y, lower_y, x_local, stacked)
        cos_b, sin_b = phase_table(upper_y, upper_y, upper_y, 1.0)
        real_part, imag_part = contract("qkxm,qb->kbxm", real_part, imag_part, cos_b, sin_b)
        twist_cos, twist_sin = phase_table(lower_y, upper_y, grid_y, 1.0)
        real_part, imag_part = rotate(
            real_part, imag_part, twist_cos[:, :, None, None], twist_sin[:, :, None, None]
        )
        cos_a, sin_a = phase_table(lower_y, lower_y, lower_y, 1.0)
        result_real, result_imag = contract("kbxm,ka->mxab", real_part, imag_part, cos_a, sin_a)
        return (
            result_real.reshape(stacked, x_local, grid_y),
            result_imag.reshape(stacked, x_local, grid_y),
        )

    split_at = 3 * planes
    potential = jnp.concatenate(
        [convolve(grid_vals[:split_at])[0], convolve(grid_vals[split_at:])[0]], axis=0
    )
    flat_pot = potential.reshape(6, cells_total)
    samples = flat_pot[:, stencil]
    forward_part = jnp.sum(samples[0:3] * sample_w[None], axis=1)
    adjoint_part = jnp.sum(samples[3:6] * spread_w[None], axis=1)
    results = jnp.concatenate([forward_part, adjoint_part], axis=0).reshape(6, devices, capacity)
    returned = lax.all_to_all(
        results, ("row", "col"), split_axis=1, concat_axis=1, tiled=True
    ).reshape(6, slots)
    homed = returned[:, position]
    block_len = near_matrix.shape[2]
    blocks = elem_count // block_len
    select = (near_list[:, :, None] == jnp.arange(blocks, dtype=jnp.int32)[None, None, :]).astype(
        jnp.float32
    )
    matrices = near_matrix.astype(jnp.float32)
    cur_blocks = currents.reshape(3, blocks, block_len)
    gathered = jnp.einsum("ctj,bnt->cbnj", cur_blocks, select, precision=exact_math)
    near_forward = jnp.einsum("cbnj,bnij->cbi", gathered, matrices, precision=exact_math)
    probe_blocks = probes.reshape(3, blocks, block_len)
    spread_back = jnp.einsum("cbi,bnij->cbnj", probe_blocks, matrices, precision=exact_math)
    near_adjoint = jnp.einsum("cbnj,bnt->ctj", spread_back, select, precision=exact_math)
    forward_out = homed[0:3] + near_forward.reshape(3, elem_count)
    adjoint_out = homed[3:6] + near_adjoint.reshape(3, elem_count)
    return (forward_out, adjoint_out)


def solution(mesh):
    return jax.shard_map(
        on_device,
        mesh=mesh,
        in_specs=(
            P(None, ("row", "col")),
            P(None, ("row", "col")),
            P(None, ("row", "col")),
            P(None, ("row", "col")),
            P(("row", "col"), None),
            P(("row", "col")),
            P(("row", "col"), None),
            P(("row", "col"), None, None, None),
            P(None, ("row", "col"), None),
        ),
        out_specs=(P(None, ("row", "col")), P(None, ("row", "col"))),
        check_vma=False,
    )
```

profile of v0, /device:TPU:0, one launch (start us, length us, event | category | flops | bytes accessed | tf_op | source)
XLA Modules:
  0.0 2775.7 jit_solution(7691777204844573677)
XLA Ops:
  1.5 9.2 reduce-window.6
  12.4 16.3 scatter_custom_fusion
  28.7 7.3 all-to-all-start
  36.7 12.8 scatter_custom_fusion.1
  53.2 6.0 all-to-all-start.1
  61.2 10.4 sort
  77.4 8.9 copy.235
  86.3 424.3 %scatter_custom_fusion.2 = f32[6,131072]{0,1:T(8,128)} fusion(s32[32768]{0:T(1024)S(1)} %get-tuple-element.10, f32[]{:T(128)} %constant.183.clone.1, f32[32768,6]{1,0:T(8,128)} %copy.235, s32[32768]{0:T(1024)S(1)} %broadcast_clamp_fusion.1), kind=kCustom, calls=%fused_computation.6 | custom fusion | flops 196608 | bytes 3146240 | tf_op jit(solution)/shard_map/scatter-add | solution.py:104
  510.7 87.3 %fusion.533 = (f32[3,131072]{0,1:T(8,128)}, f32[3,131072]{0,1:T(8,128)}) fusion(f32[6,131072]{0,1:T(8,128)} %scatter_custom_fusion.2), kind=kLoop, calls=%fused_computation.554 | loop fusion | bytes 6291456 | tf_op jit(solution)/shard_map/slice | solution.py:178
  598.0 35.5 %copy.359 = f32[3,64,32,64]{3,2,1,0:T(8,128)S(1)} copy(f32[3,64,32,64]{0,3,2,1:T(8,128)} %bitcast.50) | data formatting | bytes 3145728 | tf_op jit(solution)/shard_map/reshape | solution.py:114
  642.5 35.5 %copy.354 = f32[3,64,32,64]{3,2,1,0:T(8,128)S(1)} copy(f32[3,64,32,64]{0,3,2,1:T(8,128)} %bitcast.22) | data formatting | bytes 3145728 | tf_op jit(solution)/shard_map/reshape | solution.py:114
  681.0 6.5 subtract_bitcast_fusion.5
  687.5 10.2 fusion.32
  697.7 10.3 add_bitcast_fusion
  708.1 6.2 copy.285
  721.5 8.7 all-to-all-start.7
  730.2 10.2 fusion.34
  740.4 10.7 subtract_bitcast_fusion.1
  751.0 6.2 copy.279
  764.5 15.8 all-to-all-done.7
  783.8 10.2 fusion.50
  793.9 12.2 subtract_bitcast_fusion.4
  806.1 7.6 copy.239
  813.8 6.1 reshape.1026
  823.8 10.1 all-to-all-done.6
  839.7 10.2 fusion.48
  850.0 10.6 add_bitcast_fusion.2
  860.5 6.2 copy.245
  874.0 13.4 all-to-all-done.2
  930.3 5.1 convolution_subtract_fusion.3
  953.4 6.5 multiply_subtract_fusion.1
  959.9 11.9 fusion.24
  971.8 10.5 fusion.26
  982.3 12.1 bitcast_multiply_fusion.9
  1006.8 10.6 bitcast_multiply_fusion.8
  1020.1 6.0 convolution_subtract_fusion.2
  1045.6 5.3 all-to-all-start.9
  1051.0 5.0 fusion.88
  1056.0 5.0 convolution_subtract_fusion.1
  1070.0 10.4 fusion.40
  1080.3 12.3 bitcast_multiply_fusion.18
  1096.6 12.1 fusion.42
  1108.6 6.5 all-to-all-start.8
  1115.1 14.0 bitcast_multiply_fusion.19
  1189.0 30.0 %all-to-all-done.4 = f32[32,64,192]{2,1,0:T(8,128)} async-done(((f32[32,64,192]{2,1,0:T(8,128)}), f32[32,64,192]{2,1,0:T(8,128)}, u32[]{:S(2)}, u32[]{:S(2)}) %all-to-all-start.4) | async-done | bytes 1572896 | tf_op jit(solution)/shard_map/all_to_all | solution.py:158
  1229.5 7.3 copy.310
  1243.4 6.0 copy.306
  1253.3 5.6 reshape.1031
  1258.9 7.4 copy.266
  1282.0 5.1 convolution_subtract_fusion
  1287.1 5.0 convolution_add_fusion
  1298.7 6.0 copy.270
  1304.7 5.3 convolution_subtract_fusion.4
  1310.0 7.0 fusion.12
  1321.9 6.6 subtract_bitcast_fusion.3
  1335.0 6.8 fusion.16
  1341.9 6.5 subtract_bitcast_fusion
  1354.8 5.1 pad_maximum_fusion
  1359.9 30.2 %copy.316 = f32[6,131072]{0,1:T(8,128)} copy(f32[6,131072]{1,0:T(8,128)} %pad_maximum_fusion) | data formatting | bytes 6291456 | tf_op jit(solution)/shard_map/concatenate | solution.py:177
  1390.1 1174.7 %gather_fusion = f32[32768,6]{1,0:T(8,128)} fusion(f32[6,131072]{0,1:T(8,128)} %copy.316, s32[32768]{0:T(1024)S(1)} %broadcast_clamp_fusion), kind=kCustom, calls=%fused_computation | custom fusion | bytes 1703936 | tf_op jit(solution)/shard_map/gather | solution.py:181
  2564.8 30.7 %fusion.4 = (f32[3,8192]{0,1:T(8,128)}, f32[3,8192]{0,1:T(8,128)}) fusion(f32[6,4,8192]{0,2,1:T(8,128)} %bitcast.408, f32[4,8192]{1,0:T(4,128)S(1)} %bitcast.425, f32[4,8192]{1,0:T(4,128)S(1)} %bitcast.424), kind=kLoop, calls=%fused_computation.11 | loop fusion | flops 344064 | bytes 1245184 | tf_op jit(solution)/shard_map/reduce_sum | solution.py:182
  2602.0 138.1 %all-to-all-start.10 = ((f32[6,32,256]{2,0,1:T(8,128)}), f32[6,32,256]{2,0,1:T(8,128)S(1)}, u32[]{:S(2)}, u32[]{:S(2)}) async-start(f32[6,32,256]{2,0,1:T(8,128)} %bitcast.76), calls=%async_computation.10 | async-start | bytes 524288 | tf_op jit(solution)/shard_map/all_to_all | solution.py:185
  2740.1 5.1 convolution_bitcast_fusion
  2753.4 13.0 gather_fusion.1
  (250 shorter events, 314.3 us)
Async XLA Ops:
  0.6 11.3 copy-start.56
  0.6 35.3 %copy-start.52 = (f32[3,4096]{1,0:T(4,128)S(1)}, f32[3,4096]{1,0:T(4,128)}, u32[]{:S(2)}) copy-start(f32[3,4096]{1,0:T(4,128)} %param.10) | copy-start | bytes 147460
  0.7 35.3 %copy-start.60 = (f32[4,4096]{1,0:T(4,128)S(1)}, f32[4,4096]{1,0:T(4,128)}, u32[]{:S(2)}) copy-start(f32[4,4096]{1,0:T(4,128)} %param.11) | copy-start | bytes 196612
  0.7 35.3 %copy-start.59 = (f32[4,4096]{1,0:T(4,128)S(1)}, f32[4,4096]{1,0:T(4,128)}, u32[]{:S(2)}) copy-start(f32[4,4096]{1,0:T(4,128)} %param.12) | copy-start | bytes 196612
  0.7 35.3 %copy-start.54 = (f32[3,4096]{1,0:T(4,128)S(1)}, f32[3,4096]{1,0:T(4,128)}, u32[]{:S(2)}) copy-start(f32[3,4096]{1,0:T(4,128)} %param.9) | copy-start | bytes 147460
  12.4 37.2 %copy-start.57 = (s32[4096,1]{0,1:T(1,128)}, s32[4096,1]{0,1:T(1,128)S(1)}, u32[]{:S(2)}) copy-start(s32[4096,1]{0,1:T(1,128)S(1)} %compare_select_fusion.6) | copy-start | bytes 49156
  28.7 24.6 all-to-all-start
  53.2 22.2 all-to-all-start.1
  687.4 10.3 copy-start.5
  687.5 10.3 copy-start.10
  721.5 8.7 copy-start.6
  721.5 58.7 %all-to-all-start.7 = ((f32[32,64,192]{2,1,0:T(8,128)}), f32[32,64,192]{2,1,0:T(8,128)}, u32[]{:S(2)}, u32[]{:S(2)}) async-start(f32[32,64,192]{2,1,0:T(8,128)} %copy.286), calls=%async_computation.7 | async-start | bytes 4194304 | tf_op jit(solution)/shard_map/all_to_all | solution.py:126
  730.2 10.2 copy-start.11
  764.5 19.3 copy-start.4
  780.3 53.5 %all-to-all-start.6 = ((f32[32,64,192]{2,1,0:T(8,128)}), f32[32,64,192]{2,1,0:T(8,128)}, u32[]{:S(2)}, u32[]{:S(2)}) async-start(f32[32,64,192]{2,1,0:T(8,128)} %copy.280), calls=%async_computation.6 | async-start | bytes 4194304 | tf_op jit(solution)/shard_map/all_to_all | solution.py:125
  783.8 10.2 copy-start.8
  833.8 53.6 %all-to-all-start.2 = ((f32[32,64,192]{2,1,0:T(8,128)}), f32[32,64,192]{2,1,0:T(8,128)}, u32[]{:S(2)}, u32[]{:S(2)}) async-start(f32[32,64,192]{2,1,0:T(8,128)} %copy.240), calls=%async_computation.2 | async-start | bytes 4194304 | tf_op jit(solution)/shard_map/all_to_all | solution.py:125
  839.7 10.2 copy-start.9
  874.0 16.9 copy-start.37
  887.4 53.6 %all-to-all-start.3 = ((f32[32,64,192]{2,1,0:T(8,128)}), f32[32,64,192]{2,1,0:T(8,128)}, u32[]{:S(2)}, u32[]{:S(2)}) async-start(f32[32,64,192]{2,1,0:T(8,128)} %copy.246), calls=%async_computation.3 | async-start | bytes 4194304 | tf_op jit(solution)/shard_map/all_to_all | solution.py:126
  925.8 4.6 copy-start.16
  948.4 4.9 copy-start.30
  948.4 4.9 copy-start.33
  948.4 4.9 copy-start.34
  959.9 22.4 copy-start.20
  971.8 10.5 copy-start.22
  997.9 8.9 copy-start.27
  1002.3 4.5 copy-start.21
  1002.3 4.5 copy-start.23
  1020.1 6.0 copy-start.17
  1020.1 6.0 copy-start.28
  1029.3 3.1 copy-start.2
  1045.6 63.0 %all-to-all-start.9 = ((f32[32,64,192]{2,1,0:T(8,128)}), f32[32,64,192]{2,1,0:T(8,128)}, u32[]{:S(2)}, u32[]{:S(2)}) async-start(f32[32,64,192]{2,1,0:T(8,128)} %copy.308), calls=%async_computation.9 | async-start | bytes 4194304 | tf_op jit(solution)/shard_map/all_to_all | solution.py:159
  1050.9 5.0 copy-start.3
  1065.5 4.5 copy-start.13
  1069.9 10.4 copy-start.18
  1069.9 10.4 copy-start.24
  1108.6 6.5 copy-start.19
  1108.6 56.5 %all-to-all-start.8 = ((f32[32,64,192]{2,1,0:T(8,128)}), f32[32,64,192]{2,1,0:T(8,128)}, u32[]{:S(2)}, u32[]{:S(2)}) async-start(f32[32,64,192]{2,1,0:T(8,128)} %copy.304), calls=%async_computation.8 | async-start | bytes 4194304 | tf_op jit(solution)/shard_map/all_to_all | solution.py:158
  1135.0 3.1 copy-start.14
  1144.1 3.3 copy-start
  1160.8 8.1 copy-start.55
  1160.8 8.1 copy-start.61
  1160.8 8.4 copy-start.53
  1165.2 53.8 %all-to-all-start.4 = ((f32[32,64,192]{2,1,0:T(8,128)}), f32[32,64,192]{2,1,0:T(8,128)}, u32[]{:S(2)}, u32[]{:S(2)}) async-start(f32[32,64,192]{2,1,0:T(8,128)} %copy.264), calls=%async_computation.4 | async-start | bytes 4194304 | tf_op jit(solution)/shard_map/all_to_all | solution.py:158
  1168.9 5.2 copy-start.45
  1168.9 5.2 copy-start.47
  1168.9 5.2 copy-start.49
  1168.9 5.2 copy-start.51
  1168.9 6.0 copy-start.1
  1189.0 33.9 %copy-start.43 = (s32[4,8192,1]{1,2,0:T(1,128)S(1)}, s32[4,8192,1]{1,2,0:T(1,128)}, u32[]{:S(2)}) copy-start(s32[4,8192,1]{1,2,0:T(1,128)} %compare_select_fusion) | copy-start | bytes 393220
  1218.9 73.2 %all-to-all-start.5 = ((f32[32,64,192]{2,1,0:T(8,128)}), f32[32,64,192]{2,1,0:T(8,128)}, u32[]{:S(2)}, u32[]{:S(2)}) async-start(f32[32,64,192]{2,1,0:T(8,128)} %copy.268), calls=%async_computation.5 | async-start | bytes 4194304 | tf_op jit(solution)/shard_map/all_to_all | solution.py:159
  1269.5 3.1 copy-start.12
  1277.3 4.6 copy-start.15
  1304.7 5.3 copy-start.29
  1304.7 5.3 copy-start.31
  1304.7 5.3 copy-start.32
  1335.0 6.8 copy-start.35
  1390.1 1174.7 %copy-start.39 = (f32[4,32,256]{2,0,1:T(4,128)S(1)}, f32[4,32,256]{2,0,1:T(4,128)}, u32[]{:S(2)}) copy-start(f32[4,32,256]{2,0,1:T(4,128)} %copy-done.38) | copy-start | bytes 393220
  1390.1 1174.7 %copy-start.41 = (f32[4,32,256]{2,0,1:T(4,128)S(1)}, f32[4,32,256]{2,0,1:T(4,128)}, u32[]{:S(2)}) copy-start(f32[4,32,256]{2,0,1:T(4,128)} %copy-done.40) | copy-start | bytes 393220
  2601.2 143.9 %copy-start.42 = (f32[3,32,4,128]{3,0,2,1:T(4,128)S(1)}, f32[3,32,4,128]{3,0,2,1:T(4,128)}, u32[]{:S(2)}) copy-start(f32[3,32,4,128]{3,0,2,1:T(4,128)} %convolution_bitcast_fusion.1) | copy-start | bytes 589828
  2602.0 148.7 %all-to-all-start.10 = ((f32[6,32,256]{2,0,1:T(8,128)}), f32[6,32,256]{2,0,1:T(8,128)S(1)}, u32[]{:S(2)}, u32[]{:S(2)}) async-start(f32[6,32,256]{2,0,1:T(8,128)} %bitcast.76), calls=%async_computation.10 | async-start | bytes 524288 | tf_op jit(solution)/shard_map/all_to_all | solution.py:185
  2745.2 4.3 copy-start.58
  2771.3 3.0 copy-start.36
  (9 other events, 14.8 us)
where the time goes:
time: 2770 us; the launch traced here: 2780 us
  local copies, waits for them, and re-layouts  1640 us (59%)
  other arithmetic  490 us (18%)
  matrix products  370 us (13%)
  starting transfers between devices  190 us (7%)
  waiting for transfers between devices  79.2 us (3%)
    gather x1, local copies, waits for them, and re-layouts, on_device(): samples = flat_pot[:, stencil]  1170 us
    scatter-add x3, other arithmetic, on_device(): grid_vals = jnp.zeros((6, cells_total), jnp.float32).at[:, stencil.reshap...  435 us
    all_to_all x1, starting transfers between devices, on_device(): lax.all_to_all(results, ('row', 'col'), split_axis=1, concat_axis=1, tile...  138 us
    dot_general x16, matrix products, contract(): real_cos = jnp.einsum(pattern, real_part, cos_table, precision=exact_math)  104 us
    dot_general x14, matrix products, contract(): imag_sin = jnp.einsum(pattern, imag_part, sin_table, precision=exact_math)  93.6 us
    slice x1, local copies, waits for them, and re-layouts, on_device(): grid_vals[:split_at]  87.3 us
    dot_general x12, matrix products, contract(): imag_cos = jnp.einsum(pattern, imag_part, cos_table, precision=exact_math)  82 us
    dot_general x14, matrix products, contract(): real_sin = jnp.einsum(pattern, real_part, sin_table, precision=exact_math)  80.1 us
  transfers between devices with their start and end apart: 11, of which 8 were waited for; matrix products, arithmetic and copies ran while one was open for 14% of the time, Pallas kernels for 0%

commit v1 on v0

v1 whole, which is shorter than its diff:
```python
import math

import jax
import jax.numpy as jnp
import numpy as np
from jax import lax
from jax.experimental import pallas as pl
from jax.experimental.pallas import tpu as pltpu
from jax.sharding import PartitionSpec as P

AXES = ("row", "col")
LANES = 128
HALVES = 2
F32 = jnp.float32
BF16 = jnp.bfloat16
NT = (((1,), (1,)), ((), ()))
NN = (((1,), (0,)), ((), ()))


def split_np(table):
    hi = table.astype(np.float32).astype(jnp.bfloat16)
    lo = (table - hi.astype(np.float64)).astype(np.float32).astype(jnp.bfloat16)
    return jnp.asarray(hi), jnp.asarray(lo)


def split(x):
    hi = x.astype(BF16)
    return hi, (x - hi.astype(F32)).astype(BF16)


def dot(a, b, dims):
    return lax.dot_general(a, b, dims, preferred_element_type=F32)


def dot3(a, b, dims):
    (ah, al), (bh, bl) = a, b
    return dot(ah, bh, dims) + (dot(ah, bl, dims) + dot(al, bh, dims))


def y_table(devices, per):
    d, c, h, q, hh, cc, y = np.ix_(
        range(devices), range(2), range(HALVES), range(per), range(HALVES), range(2), range(LANES)
    )
    angle = 2.0 * math.pi * (((d * per + q) * y) % LANES) / LANES
    sine = np.where(c < cc, 1.0, -1.0) * np.sin(angle)
    value = np.where(c == cc, np.cos(angle), sine) * (h == hh)
    return value.reshape(devices * 2 * HALVES * per, HALVES * 2 * LANES)


def x_table(length, direction):
    copies = LANES // length
    c, p, x, cc, pp, k = np.ix_(
        range(2), range(copies), range(length), range(2), range(copies), range(length)
    )
    angle = direction * 2.0 * math.pi * ((x * k) % length) / length
    sine = np.where(c < cc, 1.0, -1.0) * np.sin(angle)
    value = np.where(c == cc, np.cos(angle), sine) * (p == pp)
    return value.reshape(2 * LANES, 2 * LANES)


def phases(rows, cols, length):
    turns = (np.arange(rows)[:, None] * np.arange(cols)[None, :]) % length
    angle = 2.0 * math.pi * turns / length
    return np.cos(angle), np.sin(angle)


def fft_list(re, im, direction):
    n = len(re)
    if n == 1:
        return re, im
    even_re, even_im = fft_list(re[0::2], im[0::2], direction)
    odd_re, odd_im = fft_list(re[1::2], im[1::2], direction)
    low_re, low_im, high_re, high_im = [], [], [], []
    for k in range(n // 2):
        a, b = odd_re[k], odd_im[k]
        if k == 0:
            tr, ti = a, b
        elif 4 * k == n:
            tr, ti = (-b, a) if direction > 0 else (b, -a)
        else:
            cos = math.cos(2.0 * math.pi * k / n)
            sin = direction * math.sin(2.0 * math.pi * k / n)
            tr, ti = a * cos - b * sin, a * sin + b * cos
        low_re.append(even_re[k] + tr)
        low_im.append(even_im[k] + ti)
        high_re.append(even_re[k] - tr)
        high_im.append(even_im[k] - ti)
    return low_re + high_re, low_im + high_im


def one_hot(cols, start, size):
    ids = lax.broadcasted_iota(jnp.int32, (size, cols.shape[1]), 0) + start
    return jnp.where(ids == cols, 1.0, 0.0).astype(BF16)


def project_call(field, rc, payload, yhi, ylo, tw_cos, tw_sin, x_local, grid_y):
    slots = rc.shape[1]
    n1 = grid_y // LANES
    k1l = n1 // HALVES
    rows = k1l * x_local
    width = HALVES * 2 * LANES
    build = 512
    wide = 1024
    window = 256

    def kernel(rc_ref, pay_ref, yhi_ref, ylo_ref, cos_ref, sin_ref, out_ref, v_ref, g0_ref, g1_ref, x_ref):
        half = 4 * x_local

        @pl.loop(0, slots // build)
        def _(i):
            at = pl.ds(pl.multiple_of(i * build, build), build)
            row = rc_ref[0:1, at]
            ids = lax.broadcasted_iota(jnp.int32, (x_local, build), 0)
            m0 = ids == row
            m1 = ids == row + 1
            for c in range(2):
                u = pay_ref[3 * c + field : 3 * c + field + 1, at]
                for b in range(2):
                    p0 = u * pay_ref[6 + 4 * c + b : 7 + 4 * c + b, at]
                    p1 = u * pay_ref[8 + 4 * c + b : 9 + 4 * c + b, at]
                    value = jnp.where(m0, p0, jnp.where(m1, p1, 0.0))
                    hi, lo = split(value)
                    base = (b * 2 + c) * x_local
                    v_ref[base : base + x_local, at] = hi
                    v_ref[half + base : half + base + x_local, at] = lo

        @pl.loop(0, grid_y // window)
        def _(w):
            start = pl.multiple_of(w * window, window)

            def step(i, acc):
                at = pl.ds(pl.multiple_of(i * wide, wide), wide)
                hot = one_hot(rc_ref[1:2, at], start, window)
                return acc + dot(v_ref[:, at], hot, NT)

            acc = lax.fori_loop(0, slots // wide, step, jnp.zeros((2 * half, window), F32))
            total = acc[:half] + acc[half:]
            g0_ref[:, pl.ds(start, window)] = total[: 2 * x_local]
            g1_ref[:, pl.ds(start, window)] = total[2 * x_local :]

        g0_ref[...] = g0_ref[...] + pltpu.roll(g1_ref[...], 1, 1)

        @pl.loop(0, x_local // 8)
        def _(i):
            re_at = pl.ds(pl.multiple_of(i * 8, 8), 8)
            im_at = pl.ds(pl.multiple_of(x_local + i * 8, 8), 8)
            re = [g0_ref[re_at, y * LANES : (y + 1) * LANES] for y in range(n1)]
            im = [g0_ref[im_at, y * LANES : (y + 1) * LANES] for y in range(n1)]
            re, im = fft_list(re, im, -1.0)
            for k in range(n1):
                cos, sin = cos_ref[k : k + 1, :], sin_ref[k : k + 1, :]
                to = pl.ds(pl.multiple_of((k % k1l) * x_local + i * 8, 8), 8)
                left = (k // k1l) * 2 * LANES
                x_ref[to, left : left + LANES] = re[k] * cos + im[k] * sin
                x_ref[to, left + LANES : left + 2 * LANES] = im[k] * cos - re[k] * sin

        out_ref[...] = dot3((yhi_ref[...], ylo_ref[...]), split(x_ref[...]), NT)

    return pl.pallas_call(
        kernel,
        out_shape=jax.ShapeDtypeStruct((yhi.shape[0], rows), F32),
        scratch_shapes=[
            pltpu.VMEM((8 * x_local, slots), BF16),
            pltpu.VMEM((2 * x_local, grid_y), F32),
            pltpu.VMEM((2 * x_local, grid_y), F32),
            pltpu.VMEM((rows, width), F32),
        ],
        compiler_params=pltpu.CompilerParams(vmem_limit_bytes=48 << 20),
        name="project",
    )(rc, payload, yhi, ylo, tw_cos, tw_sin)


def spectral_call(data, kernel_t, fwd, inv, tw_cos, tw_sin, devices):
    lanes = data.shape[1]
    rows = data.shape[0] // (2 * devices)

    def kernel(in_ref, kt_ref, fh_ref, fl_ref, ih_ref, il_ref, cos_ref, sin_ref, out_ref, re_ref, im_ref):
        @pl.loop(0, lanes // LANES)
        def _(t):
            at = pl.ds(pl.multiple_of(t * LANES, LANES), LANES)
            re = [in_ref[(2 * s) * rows : (2 * s + 1) * rows, at] for s in range(devices)]
            im = [in_ref[(2 * s + 1) * rows : (2 * s + 2) * rows, at] for s in range(devices)]
            re, im = fft_list(re, im, -1.0)
            for k in range(devices):
                cos, sin = cos_ref[k : k + 1, at], sin_ref[k : k + 1, at]
                re_ref[k * rows : (k + 1) * rows, at] = re[k] * cos + im[k] * sin
                im_ref[k * rows : (k + 1) * rows, at] = im[k] * cos - re[k] * sin

        for t in range(lanes // LANES):
            at = slice(t * LANES, (t + 1) * LANES)
            both = jnp.concatenate([re_ref[:, at], im_ref[:, at]], axis=1)
            spectrum = dot3(split(both), (fh_ref[...], fl_ref[...]), NN)
            factor = kt_ref[:, at]
            both = jnp.concatenate([spectrum[:, :LANES] * factor, spectrum[:, LANES:] * factor], axis=1)
            back = dot3(split(both), (ih_ref[...], il_ref[...]), NN)
            re_ref[:, at] = back[:, :LANES]
            im_ref[:, at] = back[:, LANES:]

        @pl.loop(0, lanes // LANES)
        def _(t):
            at = pl.ds(pl.multiple_of(t * LANES, LANES), LANES)
            re, im = [], []
            for k in range(devices):
                cos, sin = cos_ref[k : k + 1, at], sin_ref[k : k + 1, at]
                a = re_ref[k * rows : (k + 1) * rows, at]
                b = im_ref[k * rows : (k + 1) * rows, at]
                re.append(a * cos - b * sin)
                im.append(b * cos + a * sin)
            re, im = fft_list(re, im, 1.0)
            for s in range(devices):
                out_ref[(2 * s) * rows : (2 * s + 1) * rows, at] = re[s]
                out_ref[(2 * s + 1) * rows : (2 * s + 2) * rows, at] = im[s]

    return pl.pallas_call(
        kernel,
        out_shape=jax.ShapeDtypeStruct(data.shape, F32),
        scratch_shapes=[
            pltpu.VMEM((devices * rows, lanes), F32),
            pltpu.VMEM((devices * rows, lanes), F32),
        ],
        compiler_params=pltpu.CompilerParams(vmem_limit_bytes=48 << 20),
        name="spectral",
    )(data, kernel_t, *fwd, *inv, tw_cos, tw_sin)


def sample_call(data, rc, payload, yhi, ylo, tw_cos, tw_sin, x_local, grid_y):
    slots = rc.shape[1]
    n1 = grid_y // LANES
    k1l = n1 // HALVES
    rows = k1l * x_local
    width = HALVES * 2 * LANES
    block = 256

    def kernel(in_ref, rc_ref, pay_ref, yhi_ref, ylo_ref, cos_ref, sin_ref, out_ref, u_ref, g_ref, p_ref):
        half = 4 * x_local
        turned = jnp.transpose(in_ref[...])
        u_ref[...] = dot3(split(turned), (yhi_ref[...], ylo_ref[...]), NN)

        @pl.loop(0, x_local // 8)
        def _(i):
            re, im = [], []
            for k in range(n1):
                cos, sin = cos_ref[k : k + 1, :], sin_ref[k : k + 1, :]
                at = pl.ds(pl.multiple_of((k % k1l) * x_local + i * 8, 8), 8)
                left = (k // k1l) * 2 * LANES
                a = u_ref[at, left : left + LANES]
                b = u_ref[at, left + LANES : left + 2 * LANES]
                re.append(a * cos - b * sin)
                im.append(b * cos + a * sin)
            re, im = fft_list(re, im, 1.0)
            re_at = pl.ds(pl.multiple_of(i * 8, 8), 8)
            im_at = pl.ds(pl.multiple_of(x_local + i * 8, 8), 8)
            for y in range(n1):
                g_ref[re_at, y * LANES : (y + 1) * LANES] = re[y]
                g_ref[im_at, y * LANES : (y + 1) * LANES] = im[y]

        hi, lo = split(g_ref[...])
        p_ref[0 : 2 * x_local] = hi
        p_ref[half : half + 2 * x_local] = lo
        hi, lo = split(pltpu.roll(g_ref[...], grid_y - 1, 1))
        p_ref[2 * x_local : half] = hi
        p_ref[half + 2 * x_local :] = lo

        @pl.loop(0, slots // block)
        def _(i):
            at = pl.ds(pl.multiple_of(i * block, block), block)
            hot = one_hot(rc_ref[1:2, at], 0, grid_y)
            both = dot(p_ref[...], hot, NN)
            total = both[:half] + both[half:]
            row = rc_ref[0:1, at]
            ids = lax.broadcasted_iota(jnp.int32, (x_local, block), 0)
            m0 = ids == row
            m1 = ids == row + 1
            for c in range(2):
                result = jnp.zeros((x_local, block), F32)
                for b in range(2):
                    other = 10 - 4 * c
                    w0 = pay_ref[other + b : other + b + 1, at]
                    w1 = pay_ref[other + 2 + b : other + 3 + b, at]
                    base = (b * 2 + c) * x_local
                    weight = jnp.where(m0, w0, jnp.where(m1, w1, 0.0))
                    result = result + weight * total[base : base + x_local]
                out_ref[c : c + 1, at] = jnp.sum(result, axis=0, keepdims=True)

    return pl.pallas_call(
        kernel,
        out_shape=jax.ShapeDtypeStruct((2, slots), F32),
        scratch_shapes=[
            pltpu.VMEM((rows, width), F32),
            pltpu.VMEM((2 * x_local, grid_y), F32),
            pltpu.VMEM((8 * x_local, grid_y), BF16),
        ],
        compiler_params=pltpu.CompilerParams(vmem_limit_bytes=48 << 20),
        name="sample",
    )(data, rc, payload, yhi, ylo, tw_cos, tw_sin)


def near_terms(currents, probes, near_list, near_matrix):
    block_len = near_matrix.shape[2]
    blocks = near_list.shape[0]
    select = (near_list[:, :, None] == jnp.arange(blocks, dtype=jnp.int32)[None, None, :]).astype(F32)
    cur_blocks = currents.reshape(3, blocks, block_len)
    gathered = jnp.einsum("ctj,bnt->cbnj", cur_blocks, select, precision=lax.Precision.HIGHEST)
    g_hi, g_lo = split(gathered)
    forward = jnp.einsum(
        "cbnj,bnij->cbi", jnp.concatenate([g_hi, g_lo]), near_matrix, preferred_element_type=F32
    )
    p_hi, p_lo = split(probes.reshape(3, blocks, block_len))
    spread = jnp.einsum(
        "cbi,bnij->cbnj", jnp.concatenate([p_hi, p_lo]), near_matrix, preferred_element_type=F32
    )
    adjoint = jnp.einsum(
        "cbnj,bnt->ctj", spread[:3] + spread[3:], select, precision=lax.Precision.HIGHEST
    )
    return (forward[:3] + forward[3:]).reshape(3, -1), adjoint.reshape(3, -1)


def on_device(
    currents, probes, proj_weights, interp_weights, owner, cell, near_list, near_matrix, kernel_hat
):
    devices = lax.axis_size("row") * lax.axis_size("col")
    elem_count = currents.shape[1]
    capacity = 2 * elem_count // devices
    dz_count, ky_local, grid_x = kernel_hat.shape
    assert dz_count == 1
    grid_y = ky_local * devices
    x_local = grid_x // devices
    slots = devices * capacity
    n1 = grid_y // LANES
    per = ky_local // n1
    k1l = n1 // HALVES

    target = owner[:, 0]
    owner_ids = jnp.arange(devices, dtype=jnp.int32)
    member = (target[:, None] == owner_ids[None, :]).astype(jnp.int32)
    before = jnp.cumsum(member, axis=0) - member
    slot_index = jnp.sum(before * member, axis=1)
    position = target * capacity + slot_index
    payload = jnp.concatenate(
        [currents, probes, proj_weights, interp_weights, cell.astype(F32)[None, :]], axis=0
    )
    outgoing = jnp.zeros((15, slots), F32).at[:, position].set(payload)
    arrived = lax.all_to_all(
        outgoing.reshape(15, devices, capacity), AXES, split_axis=1, concat_axis=1, tiled=True
    ).reshape(15, slots)
    cell_in = arrived[14].astype(jnp.int32)
    rc = jnp.stack([cell_in // grid_y % (x_local - 1), cell_in % grid_y])

    yhi, ylo = split_np(y_table(devices, per))
    ty_cos, ty_sin = (jnp.asarray(t, F32) for t in phases(n1, LANES, grid_y))
    tx_cos, tx_sin = (
        jnp.asarray(np.tile(t, (1, k1l)), F32) for t in phases(devices, x_local, grid_x)
    )
    fwd, inv = split_np(x_table(x_local, -1.0)), split_np(x_table(x_local, 1.0))

    kernel_view = kernel_hat.reshape(per, HALVES, k1l, x_local, devices)
    kernel_t = jnp.transpose(kernel_view, (4, 1, 0, 2, 3)) * (1.0 / (grid_x * grid_y))
    kernel_t = kernel_t.reshape(devices * HALVES * per, k1l * x_local)

    def exchange(x):
        shaped = x.reshape(devices, 2 * HALVES * per, x.shape[1])
        moved = lax.all_to_all(shaped, AXES, split_axis=0, concat_axis=0, tiled=True)
        return moved.reshape(x.shape)

    results = []
    for field in range(3):
        spectra = project_call(
            field, rc, arrived, yhi, ylo, ty_cos, ty_sin, x_local, grid_y
        )
        spectra = exchange(spectra)
        products = spectral_call(spectra, kernel_t, fwd, inv, tx_cos, tx_sin, devices)
        products = exchange(products)
        results.append(
            sample_call(products, rc, arrived, yhi, ylo, ty_cos, ty_sin, x_local, grid_y)
        )
    stacked = jnp.concatenate(results, axis=0).reshape(6, devices, capacity)
    returned = lax.all_to_all(stacked, AXES, split_axis=1, concat_axis=1, tiled=True).reshape(6, slots)
    homed = returned[:, position]
    near_forward, near_adjoint = near_terms(currents, probes, near_list, near_matrix)
    return (homed[0::2] + near_forward, homed[1::2] + near_adjoint)


def solution(mesh):
    return jax.shard_map(
        on_device,
        mesh=mesh,
        in_specs=(
            P(None, AXES),
            P(None, AXES),
            P(None, AXES),
            P(None, AXES),
            P(AXES, None),
            P(AXES),
            P(AXES, None),
            P(AXES, None, None, None),
            P(None, AXES, None),
        ),
        out_specs=(P(None, AXES), P(None, AXES)),
        check_vma=False,
    )
```

time: 2770 us -> 426 us (0.15)
  local copies, waits for them, and re-layouts: 1640 us -> 84.7 us
  other arithmetic: 490 us -> 20.9 us
  matrix products: 370 us -> 4.75 us
  Pallas kernels: 0 us -> 200 us
  starting transfers between devices: 190 us -> 29.7 us
    gather x1 -> x0, local copies, waits for them, and re-layouts: 1170 us -> none  [on_device(): samples = flat_pot[:, stencil]]
    scatter-add x3 -> x0, other arithmetic: 435 us -> none  [on_device(): grid_vals = jnp.zeros((6, cells_total), jnp.float32).at[:, stencil.reshap...]
    dot_general x60 -> x4, matrix products: 370 us -> 4.75 us  [the longest x1 3.53 us: near_terms(): jnp.einsum('cbnj,bnij->cbi', jnp.concatenate([g_hi, g_lo]), near_matrix,...]
    pallas_call x0 -> x9, Pallas kernels: none -> 200 us  [the longest x3 114 us: project_call(): pl.pallas_call(kernel, out_shape=jax.ShapeDtypeStruct((yhi.shape[0], rows...]
    reshape x29 -> x4, local copies, waits for them, and re-layouts: 183 us -> 8.41 us  [the longest x2 4.08 us: near_terms(): return ((forward[:3] + forward[3:]).reshape(3, -1), adjoint.reshape(3, -1))]
    all_to_all x11 -> x7, starting transfers between devices: 190 us -> 29.7 us  [the longest x6 23.9 us: exchange(): lax.all_to_all(shaped, AXES, split_axis=0, concat_axis=0, tiled=True)]
    slice x6 -> x3, local copies, waits for them, and re-layouts: 88.7 us -> 16.7 us  [the longest x2 15.9 us: on_device(): return (homed[0::2] + near_forward, homed[1::2] + near_adjoint)]
    concatenate x5 -> x2, local copies, waits for them, and re-layouts: 45.2 us -> 0.98 us  [on_device(): jnp.concatenate([currents, probes, proj_weights, interp_weights, cell.ast...]
  transfers between devices with their start and end apart: 11 -> 7, of which waited for: 8 -> 4; matrix products, arithmetic and copies ran while one was open for 14% -> 4% of each run, Pallas kernels for 0% -> 32%
where the time goes in v1:
time: 426 us; the launch traced here: 425 us
  Pallas kernels  200 us (47%)
  local copies, waits for them, and re-layouts  84.7 us (20%)
  waiting for transfers between devices  60.4 us (14%)
  starting transfers between devices  29.7 us (7%)
  blocking collectives  23.5 us (6%)
  other arithmetic  20.9 us (5%)
  matrix products  4.75 us (1%)
    pallas_call x3, Pallas kernels, project_call(): pl.pallas_call(kernel, out_shape=jax.ShapeDtypeStruct((yhi.shape[0], rows...  114 us
    pallas_call x3, Pallas kernels, sample_call(): pl.pallas_call(kernel, out_shape=jax.ShapeDtypeStruct((2, slots), F32), s...  79.1 us
    all_to_all x6, waiting for transfers between devices, exchange(): lax.all_to_all(shaped, AXES, split_axis=0, concat_axis=0, tiled=True)  54.2 us
    unnamed x86, local copies, waits for them, and re-layouts  24.5 us
    all_to_all x6, starting transfers between devices, exchange(): lax.all_to_all(shaped, AXES, split_axis=0, concat_axis=0, tiled=True)  23.9 us
    all_to_all x1, blocking collectives, on_device(): lax.all_to_all(outgoing.reshape(15, devices, capacity), AXES, split_axis=...  23.5 us
    slice x2, local copies, waits for them, and re-layouts, on_device(): return (homed[0::2] + near_forward, homed[1::2] + near_adjoint)  15.9 us
    gather x1, local copies, waits for them, and re-layouts, on_device(): homed = returned[:, position]  13 us
  transfers between devices with their start and end apart: 7, of which 4 were waited for; matrix products, arithmetic and copies ran while one was open for 4% of the time, Pallas kernels for 32%

profile of v1, /device:TPU:0, one launch (start us, length us, event | category | flops | bytes accessed | tf_op | source)
XLA Modules:
  0.0 424.9 jit_solution(9163327409444950868)
XLA Ops:
  0.7 0.8 fusion.5
  1.5 9.2 %reduce-window.6 = s32[32,32,128]{2,1,0:T(8,128)S(1)} reduce-window(s32[32,32,128]{2,1,0:T(8,128)S(1)} %fusion.5, s32[]{:T(128)} %constant.61.clone.1), window={size=1x1x128 pad=0_0x0_0x127_0}, to_apply=%region_0.0 | reduce-window | flops 16646144 | bytes 1048580 | tf_op jit(solution)/shard_map/reduce-window
  10.8 0.8 slice_reduce_fusion
  12.8 0.6 copy.42
  13.5 12.8 %scatter_custom_fusion = f32[15,8192]{0,1:T(8,128)} fusion(s32[4096]{0:T(1024)S(1)} %bitcast.126, f32[4096,15]{1,0:T(8,128)S(1)} %copy.42, f32[]{:T(128)} %constant.59.clone.1), kind=kCustom, calls=%fused_computation.3 | custom fusion | bytes 491524 | tf_op jit(solution)/shard_map/scatter | solution.py:342
  26.3 2.8 copy.43
  29.2 23.5 %all_to_all.40 = f32[15,32,256]{2,0,1:T(8,128)S(1)} all-to-all(f32[15,32,256]{2,0,1:T(8,128)S(1)} %copy.43), channel_id=1, replica_groups=mesh['row'=4,'col'=8] {'row','col'}, dimensions={1} | all-to-all | bytes 983040 | tf_op jit(solution)/shard_map/all_to_all | solution.py:343
  53.8 37.9 %project.3 = f32[512,512]{1,0:T(8,128)S(1)} custom-call(s32[2,8192]{1,0:T(2,128)S(1)} %pad_add_fusion.rc_ref, f32[15,8192]{1,0:T(8,128)S(1)} %bitcast.96, bf16[512,512]{1,0:T(8,128)(2,1)S(1)} %copy-done, bf16[512,512]{1,0:T(8,128)(2,1)S(1)} %copy-done.1, f32[16,128]{1,0:T(8,128)S(1)} %copy-done.24, f32[16,128]{1,0:T(8,128)S(1)} %copy-done.25), custom_call_target="tpu_custom_call" | custom-call | tf_op jit(solution)/shard_map/project/pallas_call | solution.py:159
  91.7 1.0 copy-done.11
  92.7 2.6 all-to-all-start.1
  95.3 37.9 %project.4 = f32[512,512]{1,0:T(8,128)S(1)} custom-call(s32[2,8192]{1,0:T(2,128)S(1)} %pad_add_fusion.rc_ref, f32[15,8192]{1,0:T(8,128)S(1)} %bitcast.97, bf16[512,512]{1,0:T(8,128)(2,1)S(1)} %copy-done, bf16[512,512]{1,0:T(8,128)(2,1)S(1)} %copy-done.1, f32[16,128]{1,0:T(8,128)S(1)} %copy-done.24, f32[16,128]{1,0:T(8,128)S(1)} %copy-done.25), custom_call_target="tpu_custom_call" | custom-call | tf_op jit(solution)/shard_map/project/pallas_call | solution.py:159
  133.3 1.0 copy-done.10
  134.2 1.0 copy-done.5
  135.2 5.8 %all-to-all-start.3 = ((f32[32,16,512]{2,1,0:T(8,128)}), f32[32,16,512]{2,1,0:T(8,128)S(1)}, u32[]{:S(2)}, u32[]{:S(2)}) async-start(f32[32,16,512]{2,1,0:T(8,128)} %bitcast.110), calls=%async_computation.3 | async-start | bytes 2097152 | tf_op jit(solution)/shard_map/all_to_all | solution.py:362
  141.1 37.9 %project.5 = f32[512,512]{1,0:T(8,128)S(1)} custom-call(s32[2,8192]{1,0:T(2,128)S(1)} %pad_add_fusion.rc_ref, f32[15,8192]{1,0:T(8,128)S(1)} %bitcast.98, bf16[512,512]{1,0:T(8,128)(2,1)S(1)} %copy-done, bf16[512,512]{1,0:T(8,128)(2,1)S(1)} %copy-done.1, f32[16,128]{1,0:T(8,128)S(1)} %copy-done.24, f32[16,128]{1,0:T(8,128)S(1)} %copy-done.25), custom_call_target="tpu_custom_call" | custom-call | tf_op jit(solution)/shard_map/project/pallas_call | solution.py:159
  179.0 1.0 copy-done.9
  180.0 1.0 copy-done.3
  181.0 6.0 %all-to-all-start.5 = ((f32[32,16,512]{2,1,0:T(8,128)}), f32[32,16,512]{2,1,0:T(8,128)S(1)}, u32[]{:S(2)}, u32[]{:S(2)}) async-start(f32[32,16,512]{2,1,0:T(8,128)} %bitcast.109), calls=%async_computation.5 | async-start | bytes 2097152 | tf_op jit(solution)/shard_map/all_to_all | solution.py:362
  187.0 1.1 broadcast_multiply_fusion
  188.1 2.0 mul.27
  190.1 3.4 copy.45
  193.5 1.5 reshape.192.kt_ref
  195.1 1.2 copy-done.6
  196.3 0.9 copy-done.14
  197.2 0.9 copy-done.17
  198.1 0.8 copy-done.21
  198.9 2.3 spectral.3
  201.2 1.0 copy-done.8
  202.2 12.2 %all-to-all-done.5 = f32[32,16,512]{2,1,0:T(8,128)S(1)} async-done(((f32[32,16,512]{2,1,0:T(8,128)}), f32[32,16,512]{2,1,0:T(8,128)S(1)}, u32[]{:S(2)}, u32[]{:S(2)}) %all-to-all-start.5) | async-done | bytes 1048608 | tf_op jit(solution)/shard_map/all_to_all | solution.py:362
  214.4 3.4 all-to-all-start.2
  217.8 1.2 copy-done.4
  219.0 0.9 copy-done.15
  219.9 0.9 copy-done.18
  220.8 0.8 copy-done.22
  221.7 2.3 spectral.4
  224.0 1.0 copy-done.7
  224.9 20.4 %all-to-all-done.2 = f32[32,16,512]{2,1,0:T(8,128)} async-done(((f32[32,16,512]{2,1,0:T(8,128)}), f32[32,16,512]{2,1,0:T(8,128)}, u32[]{:S(2)}, u32[]{:S(2)}) %all-to-all-start.2) | async-done | bytes 1048608 | tf_op jit(solution)/shard_map/all_to_all | solution.py:362
  245.3 3.4 all-to-all-start.4
  248.8 0.9 copy-done.16
  249.7 0.9 copy-done.19
  250.6 0.8 copy-done.23
  251.4 2.3 spectral.5
  253.7 1.0 copy-done.2
  254.7 21.6 %all-to-all-done.4 = f32[32,16,512]{2,1,0:T(8,128)} async-done(((f32[32,16,512]{2,1,0:T(8,128)}), f32[32,16,512]{2,1,0:T(8,128)}, u32[]{:S(2)}, u32[]{:S(2)}) %all-to-all-start.4) | async-done | bytes 1048608 | tf_op jit(solution)/shard_map/all_to_all | solution.py:362
  276.3 2.6 all-to-all-start.6
  279.4 3.5 convolution_bitcast_fusion.2
  282.9 0.7 convolution_bitcast_fusion
  283.6 0.7 fusion.8
  284.2 26.8 %sample.3 = f32[2,8192]{1,0:T(2,128)S(1)} custom-call(f32[512,512]{1,0:T(8,128)} %bitcast.13.in_ref, s32[2,8192]{1,0:T(2,128)S(1)} %pad_add_fusion.rc_ref, f32[15,8192]{1,0:T(8,128)S(1)} %bitcast.99, bf16[512,512]{1,0:T(8,128)(2,1)S(1)} %copy-done, bf16[512,512]{1,0:T(8,128)(2,1)S(1)} %copy-done.1, f32[16,128]{1,0:T(8,128)S(1)} %copy-done.24, ...), custom_call_target="tpu_custom_call" | custom-call | tf_op jit(solution)/shard_map/sample/pallas_call | solution.py:285
  311.0 26.8 %sample.4 = f32[2,8192]{1,0:T(2,128)S(1)} custom-call(f32[512,512]{1,0:T(8,128)} %bitcast.17.in_ref, s32[2,8192]{1,0:T(2,128)S(1)} %pad_add_fusion.rc_ref, f32[15,8192]{1,0:T(8,128)S(1)} %bitcast.100, bf16[512,512]{1,0:T(8,128)(2,1)S(1)} %copy-done, bf16[512,512]{1,0:T(8,128)(2,1)S(1)} %copy-done.1, f32[16,128]{1,0:T(8,128)S(1)} %copy-done.24, ...), custom_call_target="tpu_custom_call" | custom-call | tf_op jit(solution)/shard_map/sample/pallas_call | solution.py:285
  337.8 25.6 %sample.5 = f32[2,8192]{1,0:T(2,128)S(1)} custom-call(f32[512,512]{1,0:T(8,128)S(1)} %bitcast.108, s32[2,8192]{1,0:T(2,128)S(1)} %pad_add_fusion.rc_ref, f32[15,8192]{1,0:T(8,128)S(1)} %bitcast.101, bf16[512,512]{1,0:T(8,128)(2,1)S(1)} %copy-done, bf16[512,512]{1,0:T(8,128)(2,1)S(1)} %copy-done.1, f32[16,128]{1,0:T(8,128)S(1)} %copy-done.24, ...), custom_call_target="tpu_custom_call" | custom-call | tf_op jit(solution)/shard_map/sample/pallas_call | solution.py:285
  363.4 0.8 pad_maximum_fusion
  364.2 5.8 %all-to-all-start.7 = ((f32[6,32,256]{2,0,1:T(8,128)}), f32[6,32,256]{2,0,1:T(8,128)S(1)}, u32[]{:S(2)}, u32[]{:S(2)}) async-start(f32[6,32,256]{2,0,1:T(8,128)} %bitcast.22), calls=%async_computation.7 | async-start | bytes 524288 | tf_op jit(solution)/shard_map/all_to_all | solution.py:377
  370.4 2.0 copy.61
  372.5 2.0 copy.50
  374.5 6.2 %all-to-all-done.7 = f32[6,32,256]{2,0,1:T(8,128)S(1)} async-done(((f32[6,32,256]{2,0,1:T(8,128)}), f32[6,32,256]{2,0,1:T(8,128)S(1)}, u32[]{:S(2)}, u32[]{:S(2)}) %all-to-all-start.7) | async-done | bytes 196640 | tf_op jit(solution)/shard_map/all_to_all | solution.py:377
  380.7 2.6 copy.47
  383.3 13.0 %gather_fusion = f32[4096,6]{1,0:T(8,128)S(1)} fusion(f32[6,8192]{0,1:T(8,128)} %bitcast.116, s32[4096]{0:T(1024)S(1)} %broadcast_clamp_fusion), kind=kCustom, calls=%fused_computation | custom fusion | bytes 212992 | tf_op jit(solution)/shard_map/gather | solution.py:378
  396.3 8.1 %slice.34 = f32[3,4096]{0,1:T(8,128)} slice(f32[6,4096]{0,1:T(8,128)S(1)} %bitcast.113), slice={[1:6:2], [0:4096:1]} | slice | bytes 98304 | tf_op jit(solution)/shard_map/slice | solution.py:380
  404.4 7.8 %slice.31 = f32[3,4096]{0,1:T(8,128)} slice(f32[6,4096]{0,1:T(8,128)S(1)} %bitcast.114), slice={[0:6:2], [0:4096:1]} | slice | bytes 98304 | tf_op jit(solution)/shard_map/slice | solution.py:380
  412.2 3.8 bitcast_add_fusion
  415.9 3.0 copy.54
  418.9 3.2 add.58
  422.1 2.8 copy.53
  (85 shorter events, 3.1 us)
Async XLA Ops:
  0.6 11.3 %copy-start.33 = (s32[4096,1]{0,1:T(1,128)S(1)}, s32[4096,1]{0,1:T(1,128)}, u32[]{:S(2)}) copy-start(s32[4096,1]{0,1:T(1,128)} %param.23) | copy-start | bytes 49156
  0.6 11.8 %copy-start.38 = (s32[4096]{0:T(1024)S(1)}, s32[4096]{0:T(1024)}, u32[]{:S(2)}) copy-start(s32[4096]{0:T(1024)} %param.24) | copy-start | bytes 49156
  0.7 11.8 %copy-start.31 = (f32[3,4096]{1,0:T(4,128)S(1)}, f32[3,4096]{1,0:T(4,128)}, u32[]{:S(2)}) copy-start(f32[3,4096]{1,0:T(4,128)} %param.19) | copy-start | bytes 147460
  0.7 11.8 %copy-start.29 = (f32[3,4096]{1,0:T(4,128)S(1)}, f32[3,4096]{1,0:T(4,128)}, u32[]{:S(2)}) copy-start(f32[3,4096]{1,0:T(4,128)} %param.20) | copy-start | bytes 147460
  0.7 11.8 %copy-start.34 = (f32[4,4096]{1,0:T(4,128)S(1)}, f32[4,4096]{1,0:T(4,128)}, u32[]{:S(2)}) copy-start(f32[4,4096]{1,0:T(4,128)} %param.21) | copy-start | bytes 196612
  0.7 11.8 %copy-start.35 = (f32[4,4096]{1,0:T(4,128)S(1)}, f32[4,4096]{1,0:T(4,128)}, u32[]{:S(2)}) copy-start(f32[4,4096]{1,0:T(4,128)} %param.22) | copy-start | bytes 196612
  12.4 13.9 %copy-start.36 = (s32[4096,1]{0,1:T(1,128)}, s32[4096,1]{0,1:T(1,128)S(1)}, u32[]{:S(2)}) copy-start(s32[4096,1]{0,1:T(1,128)S(1)} %compare_select_fusion) | copy-start | bytes 49156
  29.1 24.6 %copy-start = (bf16[512,512]{1,0:T(8,128)(2,1)S(1)}, bf16[512,512]{1,0:T(8,128)(2,1)}, u32[]{:S(2)}) copy-start(bf16[512,512]{1,0:T(8,128)(2,1)} %constant.70.clone.yhi_ref) | copy-start | bytes 1572868
  29.1 24.6 %copy-start.1 = (bf16[512,512]{1,0:T(8,128)(2,1)S(1)}, bf16[512,512]{1,0:T(8,128)(2,1)}, u32[]{:S(2)}) copy-start(bf16[512,512]{1,0:T(8,128)(2,1)} %constant.71.clone.ylo_ref) | copy-start | bytes 1572868
  29.1 24.6 %copy-start.24 = (f32[16,128]{1,0:T(8,128)S(1)}, f32[16,128]{1,0:T(8,128)}, u32[]{:S(2)}) copy-start(f32[16,128]{1,0:T(8,128)} %constant.72.clone.cos_ref) | copy-start | bytes 24580
  29.1 24.6 %copy-start.25 = (f32[16,128]{1,0:T(8,128)S(1)}, f32[16,128]{1,0:T(8,128)}, u32[]{:S(2)}) copy-start(f32[16,128]{1,0:T(8,128)} %constant.73.clone.sin_ref) | copy-start | bytes 24580
  91.7 1.0 copy-start.11
  92.7 41.6 %all-to-all-start.1 = ((f32[32,16,512]{2,1,0:T(8,128)}), f32[32,16,512]{2,1,0:T(8,128)S(1)}, u32[]{:S(2)}, u32[]{:S(2)}) async-start(f32[32,16,512]{2,1,0:T(8,128)} %bitcast.111), calls=%async_computation.1 | async-start | bytes 2097152 | tf_op jit(solution)/shard_map/all_to_all | solution.py:362
  133.2 1.0 copy-start.10
  134.2 1.0 copy-start.5
  135.2 44.7 %all-to-all-start.3 = ((f32[32,16,512]{2,1,0:T(8,128)}), f32[32,16,512]{2,1,0:T(8,128)S(1)}, u32[]{:S(2)}, u32[]{:S(2)}) async-start(f32[32,16,512]{2,1,0:T(8,128)} %bitcast.110), calls=%async_computation.3 | async-start | bytes 2097152 | tf_op jit(solution)/shard_map/all_to_all | solution.py:362
  179.0 1.0 copy-start.9
  180.0 1.0 copy-start.3
  181.0 33.4 %all-to-all-start.5 = ((f32[32,16,512]{2,1,0:T(8,128)}), f32[32,16,512]{2,1,0:T(8,128)S(1)}, u32[]{:S(2)}, u32[]{:S(2)}) async-start(f32[32,16,512]{2,1,0:T(8,128)} %bitcast.109), calls=%async_computation.5 | async-start | bytes 2097152 | tf_op jit(solution)/shard_map/all_to_all | solution.py:362
  190.1 4.9 %copy-start.12 = (bf16[256,256]{1,0:T(8,128)(2,1)S(1)}, bf16[256,256]{1,0:T(8,128)(2,1)}, u32[]{:S(2)}) copy-start(bf16[256,256]{1,0:T(8,128)(2,1)} %constant.76.clone.fh_ref) | copy-start | bytes 393220
  190.1 4.9 %copy-start.13 = (bf16[256,256]{1,0:T(8,128)(2,1)S(1)}, bf16[256,256]{1,0:T(8,128)(2,1)}, u32[]{:S(2)}) copy-start(bf16[256,256]{1,0:T(8,128)(2,1)} %constant.77.clone.fl_ref) | copy-start | bytes 393220
  190.1 4.9 %copy-start.20 = (f32[32,512]{1,0:T(8,128)S(1)}, f32[32,512]{1,0:T(8,128)}, u32[]{:S(2)}) copy-start(f32[32,512]{1,0:T(8,128)} %constant.74.clone.cos_ref) | copy-start | bytes 196612
  195.1 1.2 copy-start.6
  196.3 0.9 copy-start.14
  197.2 0.9 copy-start.17
  198.1 0.8 copy-start.21
  201.2 1.0 copy-start.8
  214.4 31.0 %all-to-all-start.2 = ((f32[32,16,512]{2,1,0:T(8,128)}), f32[32,16,512]{2,1,0:T(8,128)}, u32[]{:S(2)}, u32[]{:S(2)}) async-start(f32[32,16,512]{2,1,0:T(8,128)} %bitcast.107), calls=%async_computation.2 | async-start | bytes 2097152 | tf_op jit(solution)/shard_map/all_to_all | solution.py:362
  217.8 1.2 copy-start.4
  219.0 0.9 copy-start.15
  219.9 0.9 copy-start.18
  220.8 0.8 copy-start.22
  224.0 1.0 copy-start.7
  245.3 31.0 %all-to-all-start.4 = ((f32[32,16,512]{2,1,0:T(8,128)}), f32[32,16,512]{2,1,0:T(8,128)}, u32[]{:S(2)}, u32[]{:S(2)}) async-start(f32[32,16,512]{2,1,0:T(8,128)} %bitcast.106), calls=%async_computation.4 | async-start | bytes 2097152 | tf_op jit(solution)/shard_map/all_to_all | solution.py:362
  248.7 0.9 copy-start.16
  249.7 0.9 copy-start.19
  250.6 0.8 copy-start.23
  253.7 1.0 copy-start.2
  254.7 24.3 %copy-start.32 = (f32[3,4096]{1,0:T(4,128)S(1)}, f32[3,4096]{1,0:T(4,128)}, u32[]{:S(2)}) copy-start(f32[3,4096]{1,0:T(4,128)} %param.19) | copy-start | bytes 147460
  254.7 24.3 %copy-start.39 = (s32[32,4]{0,1:T(4,128)S(1)}, s32[32,4]{0,1:T(4,128)}, u32[]{:S(2)}) copy-start(s32[32,4]{0,1:T(4,128)} %param.25) | copy-start | bytes 1540
  254.7 24.6 %copy-start.30 = (f32[3,4096]{1,0:T(4,128)S(1)}, f32[3,4096]{1,0:T(4,128)}, u32[]{:S(2)}) copy-start(f32[3,4096]{1,0:T(4,128)} %param.20) | copy-start | bytes 147460
  276.3 61.5 %all-to-all-start.6 = ((f32[32,16,512]{2,1,0:T(8,128)}), f32[32,16,512]{2,1,0:T(8,128)S(1)}, u32[]{:S(2)}, u32[]{:S(2)}) async-start(f32[32,16,512]{2,1,0:T(8,128)} %bitcast.103), calls=%async_computation.6 | async-start | bytes 2097152 | tf_op jit(solution)/shard_map/all_to_all | solution.py:362
  279.3 3.5 copy-start.26
  337.8 32.3 %copy-start.40 = (s32[32,4]{0,1:T(4,128)S(1)}, s32[32,4]{0,1:T(4,128)}, u32[]{:S(2)}) copy-start(s32[32,4]{0,1:T(4,128)} %param.25) | copy-start | bytes 1540
  363.4 9.1 %copy-start.28 = (f32[3,4096]{1,0:T(4,128)S(1)}, f32[3,4096]{1,0:T(4,128)}, u32[]{:S(2)}) copy-start(f32[3,4096]{1,0:T(4,128)} %fusion.8) | copy-start | bytes 147460
  364.2 16.5 %all-to-all-start.7 = ((f32[6,32,256]{2,0,1:T(8,128)}), f32[6,32,256]{2,0,1:T(8,128)S(1)}, u32[]{:S(2)}, u32[]{:S(2)}) async-start(f32[6,32,256]{2,0,1:T(8,128)} %bitcast.22), calls=%async_computation.7 | async-start | bytes 524288 | tf_op jit(solution)/shard_map/all_to_all | solution.py:377
  370.4 4.1 copy-start.37
  415.9 3.0 copy-start.27

commit v2 on v1

--- a/solution.py
+++ b/solution.py
@@ -11,6 +11,9 @@
 AXES = ("row", "col")
 LANES = 128
 HALVES = 2
+GROUP = 8
+CHUNK = 512
+WINDOW = 256
 F32 = jnp.float32
 BF16 = jnp.bfloat16
 NT = (((1,), (1,)), ((), ()))
@@ -93,59 +96,229 @@
     return jnp.where(ids == cols, 1.0, 0.0).astype(BF16)
 
 
-def project_call(field, rc, payload, yhi, ylo, tw_cos, tw_sin, x_local, grid_y):
+def call(kernel, name, out_shape, args, scratch=(), smem_in=(), smem_out=(), flops=0, after=()):
+    if after:
+        count, inner = len(args), kernel
+        kernel = lambda *refs: inner(*refs[:count], *refs[count + len(after) :])
+    spaces = [pltpu.SMEM if i in smem_in else pltpu.VMEM for i in range(len(args))]
+    outs = [pltpu.SMEM if i in smem_out else pltpu.VMEM for i in range(len(out_shape))]
+    moved = sum(math.prod(x.shape) * x.dtype.itemsize for x in (*args, *out_shape))
+    return pl.pallas_call(
+        kernel,
+        out_shape=list(out_shape),
+        in_specs=[pl.BlockSpec(memory_space=space) for space in spaces]
+        + [pl.BlockSpec(memory_space=pl.ANY)] * len(after),
+        out_specs=[pl.BlockSpec(memory_space=space) for space in outs],
+        scratch_shapes=list(scratch),
+        compiler_params=pltpu.CompilerParams(vmem_limit_bytes=48 << 20),
+        cost_estimate=pl.CostEstimate(flops=flops, transcendentals=0, bytes_accessed=moved),
+        name=name,
+    )(*args, *after)
+
+
+def shape(dims, dtype=F32):
+    return jax.ShapeDtypeStruct(dims, dtype)
+
+
+def expand_call(starts, keys, rows, devices, capacity, codes):
+    count = keys.shape[1]
+    wide = -(-capacity // LANES) * LANES + LANES
+    height = 16
+
+    def kernel(starts_ref, key_ref, *refs):
+        row_refs, out_ref, s_ref = refs[:-2], refs[-2], refs[-1]
+        s_ref[:, count:] = jnp.zeros((height, wide), F32)
+        for i, ref in enumerate(row_refs):
+            s_ref[i : i + 1, 0:count] = ref[...]
+        s_ref[height - 1 : height, 0:count] = (key_ref[...] & (codes - 1)).astype(F32)
+        lane = lax.broadcasted_iota(jnp.int32, (height, wide), 1)
+        free = jnp.where(lax.broadcasted_iota(jnp.int32, (height, wide), 0) == height - 1, -1.0, 0.0)
+
+        @pl.loop(0, devices)
+        def _(d):
+            first = starts_ref[d]
+            held = starts_ref[d + 1] - first
+            tile = first // LANES
+            block = s_ref[:, pl.ds(pl.multiple_of(tile * LANES, LANES), wide)]
+            moved = pltpu.roll(block, wide - (first - tile * LANES), 1)
+            out_ref[d] = jnp.where(lane < held, moved, free)[:, :capacity]
+
+    (out,) = call(
+        kernel,
+        "expand",
+        [shape((devices, height, capacity))],
+        [starts, keys, *rows],
+        scratch=[pltpu.VMEM((height, count + wide), F32)],
+        smem_in=(0,),
+    )
+    return out
+
+
+def compact_call(starts, data, count):
+    devices, height, capacity = data.shape
+    wide = -(-capacity // LANES) * LANES + LANES
+
+    def kernel(starts_ref, in_ref, out_ref, s_ref):
+        lane = lax.broadcasted_iota(jnp.int32, (height, wide), 1)
+
+        @pl.loop(0, devices)
+        def _(d):
+            first = starts_ref[d]
+            held = starts_ref[d + 1] - first
+            tile = first // LANES
+            shift = first - tile * LANES
+            at = pl.ds(pl.multiple_of(tile * LANES, LANES), wide)
+            filler = jnp.zeros((height, wide - capacity), F32)
+            moved = pltpu.roll(jnp.concatenate([in_ref[d], filler], axis=1), shift, 1)
+            keep = (lane >= shift) & (lane < shift + held)
+            s_ref[:, at] = jnp.where(keep, moved, s_ref[:, at])
+
+        out_ref[...] = s_ref[:, :count]
+
+    (out,) = call(
+        kernel,
+        "compact",
+        [shape((height, count))],
+        [starts, data],
+        scratch=[pltpu.VMEM((height, count + wide), F32)],
+        smem_in=(0,),
+    )
+    return out
+
+
+def turn_blocks(parts):
+    parts = list(parts)
+    block = lax.broadcasted_iota(jnp.int32, parts[0].shape, 1) // GROUP
+    for m in (1, 2, 4, 8):
+        high = (block & m) != 0
+        for i in range(16):
+            if i & m == 0:
+                a, b = parts[i], parts[i + m]
+                parts[i] = jnp.where(high, pltpu.roll(b, m * GROUP, 1), a)
+                parts[i + m] = jnp.where(high, b, pltpu.roll(a, LANES - m * GROUP, 1))
+    return parts
+
+
+def gather_groups(arrived, x_local, chunk):
+    devices, height, capacity = arrived.shape
+    slots = devices * capacity
+    chunks = slots // chunk
+    shift = x_local.bit_length() - 1
+    none = 1 << 20
+
+    def decode(code):
+        return code & (x_local - 1), lax.shift_right_arithmetic(code, shift)
+
+    if capacity % LANES or devices % 16:
+        turned = arrived.reshape(devices, height, capacity // GROUP, GROUP)
+        turned = jnp.transpose(turned, (1, 2, 0, 3)).reshape(height, slots)
+        row, col = decode(turned[height - 1].astype(jnp.int32))
+        per_chunk = col.reshape(chunks, chunk)
+        low = jnp.min(jnp.where(per_chunk < 0, none, per_chunk), axis=1)
+        return turned, jnp.stack([row, col]), jnp.stack([low, jnp.max(per_chunk, axis=1)])
+
+    def kernel(in_ref, out_ref, rc_ref, bound_ref):
+        @pl.loop(0, devices // 16)
+        def _(sb):
+            for t in range(capacity // LANES):
+                lanes = slice(t * LANES, (t + 1) * LANES)
+                parts = turn_blocks([in_ref[sb * 16 + i, :, lanes] for i in range(16)])
+                for j in range(16):
+                    left = (t * 16 + j) * devices * GROUP
+                    at = pl.ds(pl.multiple_of(left + sb * LANES, LANES), LANES)
+                    out_ref[:, at] = parts[j]
+                    row, col = decode(parts[j][height - 1 :].astype(jnp.int32))
+                    rc_ref[0:1, at] = row
+                    rc_ref[1:2, at] = col
+
+        @pl.loop(0, chunks)
+        def _(i):
+            col = rc_ref[1:2, pl.ds(pl.multiple_of(i * chunk, chunk), chunk)]
+            bound_ref[0, i] = jnp.min(jnp.where(col < 0, none, col))
+            bound_ref[1, i] = jnp.max(col)
+
+    return call(
+        kernel,
+        "groups",
+        [shape((height, slots)), shape((2, slots), jnp.int32), shape((2, chunks), jnp.int32)],
+        [arrived],
+        smem_out=(2,),
+    )
+
+
+def scatter_groups(results, devices, capacity):
+    height = results.shape[0]
+    if capacity % LANES or devices % 16:
+        turned = results.reshape(height, capacity // GROUP, devices, GROUP)
+        return jnp.transpose(turned, (2, 0, 1, 3)).reshape(devices, height, capacity)
+
+    def kernel(in_ref, out_ref):
+        @pl.loop(0, devices // 16)
+        def _(sb):
+            for t in range(capacity // LANES):
+                parts = []
+                for j in range(16):
+                    left = (t * 16 + j) * devices * GROUP
+                    parts.append(in_ref[:, pl.ds(pl.multiple_of(left + sb * LANES, LANES), LANES)])
+                for i, part in enumerate(turn_blocks(parts)):
+                    out_ref[sb * 16 + i, :, t * LANES : (t + 1) * LANES] = part
+
+    (out,) = call(kernel, "ungroup", [shape((devices, height, capacity))], [results])
+    return out
+
+
+def window_count(bound_ref, i):
+    first = bound_ref[0, i] // LANES
+    return first, (bound_ref[1, i] - first * LANES) // WINDOW + 1
+
+
+def project_call(field, bounds, rc, payload, yhi, ylo, tw_cos, tw_sin, x_local, grid_y, after):
     slots = rc.shape[1]
+    chunks = bounds.shape[1]
+    chunk = slots // chunks
     n1 = grid_y // LANES
     k1l = n1 // HALVES
     rows = k1l * x_local
     width = HALVES * 2 * LANES
-    build = 512
-    wide = 1024
-    window = 256
-
-    def kernel(rc_ref, pay_ref, yhi_ref, ylo_ref, cos_ref, sin_ref, out_ref, v_ref, g0_ref, g1_ref, x_ref):
-        half = 4 * x_local
-
-        @pl.loop(0, slots // build)
+    half = 4 * x_local
+
+    def kernel(bound_ref, rc_ref, pay_ref, yhi_ref, ylo_ref, cos_ref, sin_ref, out_ref, v_ref, acc_ref, g_ref, x_ref):
+        acc_ref[...] = jnp.zeros(acc_ref.shape, F32)
+
+        @pl.loop(0, chunks)
         def _(i):
-            at = pl.ds(pl.multiple_of(i * build, build), build)
-            row = rc_ref[0:1, at]
-            ids = lax.broadcasted_iota(jnp.int32, (x_local, build), 0)
-            m0 = ids == row
-            m1 = ids == row + 1
+            at = pl.ds(pl.multiple_of(i * chunk, chunk), chunk)
+            ids = lax.broadcasted_iota(jnp.int32, (x_local, chunk), 0)
+            m0 = ids == rc_ref[0:1, at]
+            m1 = ids == rc_ref[0:1, at] + 1
             for c in range(2):
                 u = pay_ref[3 * c + field : 3 * c + field + 1, at]
                 for b in range(2):
                     p0 = u * pay_ref[6 + 4 * c + b : 7 + 4 * c + b, at]
                     p1 = u * pay_ref[8 + 4 * c + b : 9 + 4 * c + b, at]
-                    value = jnp.where(m0, p0, jnp.where(m1, p1, 0.0))
-                    hi, lo = split(value)
+                    hi, lo = split(jnp.where(m0, p0, jnp.where(m1, p1, 0.0)))
                     base = (b * 2 + c) * x_local
-                    v_ref[base : base + x_local, at] = hi
-                    v_ref[half + base : half + base + x_local, at] = lo
-
-        @pl.loop(0, grid_y // window)
-        def _(w):
-            start = pl.multiple_of(w * window, window)
-
-            def step(i, acc):
-                at = pl.ds(pl.multiple_of(i * wide, wide), wide)
-                hot = one_hot(rc_ref[1:2, at], start, window)
-                return acc + dot(v_ref[:, at], hot, NT)
-
-            acc = lax.fori_loop(0, slots // wide, step, jnp.zeros((2 * half, window), F32))
-            total = acc[:half] + acc[half:]
-            g0_ref[:, pl.ds(start, window)] = total[: 2 * x_local]
-            g1_ref[:, pl.ds(start, window)] = total[2 * x_local :]
-
-        g0_ref[...] = g0_ref[...] + pltpu.roll(g1_ref[...], 1, 1)
+                    v_ref[base : base + x_local, :] = hi
+                    v_ref[half + base : half + base + x_local, :] = lo
+            first, windows = window_count(bound_ref, i)
+
+            def step(w, carry):
+                start = first * LANES + w * WINDOW
+                to = pl.ds(pl.multiple_of(start, LANES), WINDOW)
+                acc_ref[:, to] += dot(v_ref[...], one_hot(rc_ref[1:2, at], start, WINDOW), NT)
+                return carry
+
+            lax.fori_loop(0, windows, step, 0)
+
+        total = acc_ref[:half, :grid_y] + acc_ref[half:, :grid_y]
+        g_ref[...] = total[: 2 * x_local] + pltpu.roll(total[2 * x_local :], 1, 1)
 
         @pl.loop(0, x_local // 8)
         def _(i):
             re_at = pl.ds(pl.multiple_of(i * 8, 8), 8)
             im_at = pl.ds(pl.multiple_of(x_local + i * 8, 8), 8)
-            re = [g0_ref[re_at, y * LANES : (y + 1) * LANES] for y in range(n1)]
-            im = [g0_ref[im_at, y * LANES : (y + 1) * LANES] for y in range(n1)]
+            re = [g_ref[re_at, y * LANES : (y + 1) * LANES] for y in range(n1)]
+            im = [g_ref[im_at, y * LANES : (y + 1) * LANES] for y in range(n1)]
             re, im = fft_list(re, im, -1.0)
             for k in range(n1):
                 cos, sin = cos_ref[k : k + 1, :], sin_ref[k : k + 1, :]
@@ -156,21 +329,25 @@
 
         out_ref[...] = dot3((yhi_ref[...], ylo_ref[...]), split(x_ref[...]), NT)
 
-    return pl.pallas_call(
+    (out,) = call(
         kernel,
-        out_shape=jax.ShapeDtypeStruct((yhi.shape[0], rows), F32),
-        scratch_shapes=[
-            pltpu.VMEM((8 * x_local, slots), BF16),
-            pltpu.VMEM((2 * x_local, grid_y), F32),
+        "project",
+        [shape((yhi.shape[0], rows))],
+        [bounds, rc, payload, yhi, ylo, tw_cos, tw_sin],
+        scratch=[
+            pltpu.VMEM((2 * half, chunk), BF16),
+            pltpu.VMEM((2 * half, grid_y + WINDOW), F32),
             pltpu.VMEM((2 * x_local, grid_y), F32),
             pltpu.VMEM((rows, width), F32),
         ],
-        compiler_params=pltpu.CompilerParams(vmem_limit_bytes=48 << 20),
-        name="project",
-    )(rc, payload, yhi, ylo, tw_cos, tw_sin)
-
-
-def spectral_call(data, kernel_t, fwd, inv, tw_cos, tw_sin, devices):
+        smem_in=(0,),
+        flops=4 * half * slots * grid_y,
+        after=after,
+    )
+    return out
+
+
+def spectral_call(data, kernel_t, fwd, inv, tw_cos, tw_sin, devices, after):
     lanes = data.shape[1]
     rows = data.shape[0] // (2 * devices)
 
@@ -211,28 +388,32 @@
                 out_ref[(2 * s) * rows : (2 * s + 1) * rows, at] = re[s]
                 out_ref[(2 * s + 1) * rows : (2 * s + 2) * rows, at] = im[s]
 
-    return pl.pallas_call(
+    (out,) = call(
         kernel,
-        out_shape=jax.ShapeDtypeStruct(data.shape, F32),
-        scratch_shapes=[
+        "spectral",
+        [shape(data.shape)],
+        [data, kernel_t, *fwd, *inv, tw_cos, tw_sin],
+        scratch=[
             pltpu.VMEM((devices * rows, lanes), F32),
             pltpu.VMEM((devices * rows, lanes), F32),
         ],
-        compiler_params=pltpu.CompilerParams(vmem_limit_bytes=48 << 20),
-        name="spectral",
-    )(data, kernel_t, *fwd, *inv, tw_cos, tw_sin)
-
-
-def sample_call(data, rc, payload, yhi, ylo, tw_cos, tw_sin, x_local, grid_y):
+        flops=1 << 30,
+        after=after,
+    )
+    return out
+
+
+def sample_call(data, bounds, rc, payload, yhi, ylo, tw_cos, tw_sin, x_local, grid_y, after):
     slots = rc.shape[1]
     n1 = grid_y // LANES
     k1l = n1 // HALVES
     rows = k1l * x_local
     width = HALVES * 2 * LANES
-    block = 256
-
-    def kernel(in_ref, rc_ref, pay_ref, yhi_ref, ylo_ref, cos_ref, sin_ref, out_ref, u_ref, g_ref, p_ref):
-        half = 4 * x_local
+    chunks = bounds.shape[1]
+    chunk = slots // chunks
+    half = 4 * x_local
+
+    def kernel(in_ref, bound_ref, rc_ref, pay_ref, yhi_ref, ylo_ref, cos_ref, sin_ref, out_ref, u_ref, g_ref, p_ref, t_ref):
         turned = jnp.transpose(in_ref[...])
         u_ref[...] = dot3(split(turned), (yhi_ref[...], ylo_ref[...]), NN)
 
@@ -255,24 +436,32 @@
                 g_ref[im_at, y * LANES : (y + 1) * LANES] = im[y]
 
         hi, lo = split(g_ref[...])
-        p_ref[0 : 2 * x_local] = hi
-        p_ref[half : half + 2 * x_local] = lo
+        p_ref[0 : 2 * x_local, :grid_y] = hi
+        p_ref[half : half + 2 * x_local, :grid_y] = lo
         hi, lo = split(pltpu.roll(g_ref[...], grid_y - 1, 1))
-        p_ref[2 * x_local : half] = hi
-        p_ref[half + 2 * x_local :] = lo
-
-        @pl.loop(0, slots // block)
+        p_ref[2 * x_local : half, :grid_y] = hi
+        p_ref[half + 2 * x_local :, :grid_y] = lo
+        p_ref[:, grid_y:] = jnp.zeros((2 * half, WINDOW), BF16)
+
+        @pl.loop(0, chunks)
         def _(i):
-            at = pl.ds(pl.multiple_of(i * block, block), block)
-            hot = one_hot(rc_ref[1:2, at], 0, grid_y)
-            both = dot(p_ref[...], hot, NN)
-            total = both[:half] + both[half:]
-            row = rc_ref[0:1, at]
-            ids = lax.broadcasted_iota(jnp.int32, (x_local, block), 0)
-            m0 = ids == row
-            m1 = ids == row + 1
+            at = pl.ds(pl.multiple_of(i * chunk, chunk), chunk)
+            first, windows = window_count(bound_ref, i)
+            t_ref[...] = jnp.zeros(t_ref.shape, F32)
+
+            def step(w, carry):
+                start = first * LANES + w * WINDOW
+                of = pl.ds(pl.multiple_of(start, LANES), WINDOW)
+                t_ref[...] += dot(p_ref[:, of], one_hot(rc_ref[1:2, at], start, WINDOW), NN)
+                return carry
+
+            lax.fori_loop(0, windows, step, 0)
+            total = t_ref[:half] + t_ref[half:]
+            ids = lax.broadcasted_iota(jnp.int32, (x_local, chunk), 0)
+            m0 = ids == rc_ref[0:1, at]
+            m1 = ids == rc_ref[0:1, at] + 1
             for c in range(2):
-                result = jnp.zeros((x_local, block), F32)
+                result = jnp.zeros((x_local, chunk), F32)
                 for b in range(2):
                     other = 10 - 4 * c
                     w0 = pay_ref[other + b : other + b + 1, at]
@@ -282,17 +471,27 @@
                     result = result + weight * total[base : base + x_local]
                 out_ref[c : c + 1, at] = jnp.sum(result, axis=0, keepdims=True)
 
-    return pl.pallas_call(
+    (out,) = call(
         kernel,
-        out_shape=jax.ShapeDtypeStruct((2, slots), F32),
-        scratch_shapes=[
+        "sample",
+        [shape((2, slots))],
+        [data, bounds, rc, payload, yhi, ylo, tw_cos, tw_sin],
+        scratch=[
             pltpu.VMEM((rows, width), F32),
             pltpu.VMEM((2 * x_local, grid_y), F32),
-            pltpu.VMEM((8 * x_local, grid_y), BF16),
+            pltpu.VMEM((2 * half, grid_y + WINDOW), BF16),
+            pltpu.VMEM((2 * half, chunk), F32),
         ],
-        compiler_params=pltpu.CompilerParams(vmem_limit_bytes=48 << 20),
-        name="sample",
-    )(data, rc, payload, yhi, ylo, tw_cos, tw_sin)
+        smem_in=(1,),
+        flops=4 * half * slots * grid_y,
+        after=after,
+    )
+    return out
+
+
+def split_outside(x):
+    hi = lax.reduce_precision(x, 8, 7)
+    return hi.astype(BF16), (x - hi).astype(BF16)
 
 
 def near_terms(currents, probes, near_list, near_matrix):
@@ -301,11 +500,11 @@
     select = (near_list[:, :, None] == jnp.arange(blocks, dtype=jnp.int32)[None, None, :]).astype(F32)
     cur_blocks = currents.reshape(3, blocks, block_len)
     gathered = jnp.einsum("ctj,bnt->cbnj", cur_blocks, select, precision=lax.Precision.HIGHEST)
-    g_hi, g_lo = split(gathered)
+    g_hi, g_lo = split_outside(gathered)
     forward = jnp.einsum(
         "cbnj,bnij->cbi", jnp.concatenate([g_hi, g_lo]), near_matrix, preferred_element_type=F32
     )
-    p_hi, p_lo = split(probes.reshape(3, blocks, block_len))
+    p_hi, p_lo = split_outside(probes.reshape(3, blocks, block_len))
     spread = jnp.einsum(
         "cbi,bnij->cbnj", jnp.concatenate([p_hi, p_lo]), near_matrix, preferred_element_type=F32
     )
@@ -330,21 +529,22 @@
     per = ky_local // n1
     k1l = n1 // HALVES
 
+    codes = x_local * grid_y
+    assert codes & (codes - 1) == 0
+
     target = owner[:, 0]
-    owner_ids = jnp.arange(devices, dtype=jnp.int32)
-    member = (target[:, None] == owner_ids[None, :]).astype(jnp.int32)
-    before = jnp.cumsum(member, axis=0) - member
-    slot_index = jnp.sum(before * member, axis=1)
-    position = target * capacity + slot_index
-    payload = jnp.concatenate(
-        [currents, probes, proj_weights, interp_weights, cell.astype(F32)[None, :]], axis=0
-    )
-    outgoing = jnp.zeros((15, slots), F32).at[:, position].set(payload)
-    arrived = lax.all_to_all(
-        outgoing.reshape(15, devices, capacity), AXES, split_axis=1, concat_axis=1, tiled=True
-    ).reshape(15, slots)
-    cell_in = arrived[14].astype(jnp.int32)
-    rc = jnp.stack([cell_in // grid_y % (x_local - 1), cell_in % grid_y])
+    row, col = cell // grid_y % (x_local - 1), cell % grid_y
+    key = target * codes + col * x_local + row
+    columns = [*currents, *probes, *proj_weights, *interp_weights]
+    order = lax.iota(jnp.int32, elem_count)
+    key, *columns, order = lax.sort((key, *columns, order), num_keys=1, is_stable=False)
+    bounds_of = jnp.arange(devices + 1, dtype=jnp.int32)
+    starts = jnp.sum((target[None, :] < bounds_of[:, None]).astype(jnp.int32), axis=1)
+    outgoing = expand_call(
+        starts, key[None, :], [x[None, :] for x in columns], devices, capacity, codes
+    )
+    arrived = lax.all_to_all(outgoing, AXES, split_axis=0, concat_axis=0, tiled=True)
+    payload, rc, bounds = gather_groups(arrived, x_local, CHUNK)
 
     yhi, ylo = split_np(y_table(devices, per))
     ty_cos, ty_sin = (jnp.asarray(t, F32) for t in phases(n1, LANES, grid_y))
@@ -362,22 +562,33 @@
         moved = lax.all_to_all(shaped, AXES, split_axis=0, concat_axis=0, tiled=True)
         return moved.reshape(x.shape)
 
-    results = []
+    def sample(products, *after):
+        return sample_call(
+            products, bounds, rc, payload, yhi, ylo, ty_cos, ty_sin, x_local, grid_y, after
+        )
+
+    def spectral(spectra, *after):
+        return exchange(spectral_call(spectra, kernel_t, fwd, inv, tx_cos, tx_sin, devices, after))
+
+    spectra, after = [], ()
     for field in range(3):
-        spectra = project_call(
-            field, rc, arrived, yhi, ylo, ty_cos, ty_sin, x_local, grid_y
+        grids = project_call(
+            field, bounds, rc, payload, yhi, ylo, ty_cos, ty_sin, x_local, grid_y, after
         )
-        spectra = exchange(spectra)
-        products = spectral_call(spectra, kernel_t, fwd, inv, tx_cos, tx_sin, devices)
-        products = exchange(products)
-        results.append(
-            sample_call(products, rc, arrived, yhi, ylo, ty_cos, ty_sin, x_local, grid_y)
-        )
-    stacked = jnp.concatenate(results, axis=0).reshape(6, devices, capacity)
-    returned = lax.all_to_all(stacked, AXES, split_axis=1, concat_axis=1, tiled=True).reshape(6, slots)
-    homed = returned[:, position]
+        spectra.append(exchange(grids))
+        after = (grids,)
+    products = [spectral(spectra[0]), spectral(spectra[1])]
+    first = sample(products[0])
+    products.append(spectral(spectra[2], first))
+    second = sample(products[1])
+    third = sample(products[2], second)
+    results = [first, second, third]
+    returning = scatter_groups(jnp.concatenate(results, axis=0), devices, capacity)
+    returned = lax.all_to_all(returning, AXES, split_axis=0, concat_axis=0, tiled=True)
+    homed = compact_call(starts, returned, elem_count)
+    _, *homed = lax.sort((order, *homed), num_keys=1, is_stable=False)
     near_forward, near_adjoint = near_terms(currents, probes, near_list, near_matrix)
-    return (homed[0::2] + near_forward, homed[1::2] + near_adjoint)
+    return (jnp.stack(homed[0::2]) + near_forward, jnp.stack(homed[1::2]) + near_adjoint)
 
 
 def solution(mesh):

time: 426 us -> 326 us (0.77)
  Pallas kernels: 200 us -> 115 us
  local copies, waits for them, and re-layouts: 84.7 us -> 33.9 us
  blocking collectives: 23.5 us -> 64.7 us
    pallas_call x9 -> x13, Pallas kernels: 200 us -> 115 us  [call(): pl.pallas_call(kernel, out_shape=list(out_shape), in_specs=[pl.BlockSpec(...]
    all_to_all x1 -> x2, blocking collectives: 23.5 us -> 64.7 us  [the longest x1 41.2 us: exchange(): lax.all_to_all(shaped, AXES, split_axis=0, concat_axis=0, tiled=True)]
    slice x3 -> x0, local copies, waits for them, and re-layouts: 16.7 us -> none  [the longest x2 15.9 us: on_device(): return (homed[0::2] + near_forward, homed[1::2] + near_adjoint)]
    gather x1 -> x0, local copies, waits for them, and re-layouts: 13 us -> none  [on_device(): homed = returned[:, position]]
    scatter x1 -> x0, local copies, waits for them, and re-layouts: 12.8 us -> none  [on_device(): outgoing = jnp.zeros((15, slots), F32).at[:, position].set(payload)]
    sort x0 -> x2, other arithmetic: none -> 11.6 us  [the longest x1 5.99 us: on_device(): lax.sort((key, *columns, order), num_keys=1, is_stable=False)]
    another operation x4 -> x0, other arithmetic: 9.67 us -> none
    reshape x3 -> x0, local copies, waits for them, and re-layouts: 6.92 us -> none  [the longest x2 4.08 us: near_terms(): return ((forward[:3] + forward[3:]).reshape(3, -1), adjoint.reshape(3, -1))]
  transfers between devices with their start and end apart: 7 -> 6, of which waited for: 4 -> 6; matrix products, arithmetic and copies ran while one was open for 4% -> 6% of each run, Pallas kernels for 32% -> 17%
where the time goes in v2:
time: 326 us; the launch traced here: 323 us
  Pallas kernels  115 us (35%)
  blocking collectives  64.7 us (20%)
  waiting for transfers between devices  56.9 us (17%)
  local copies, waits for them, and re-layouts  33.9 us (10%)
  starting transfers between devices  25.9 us (8%)
  other arithmetic  18.4 us (6%)
  matrix products  6.93 us (2%)
    pallas_call x13, Pallas kernels, call(): pl.pallas_call(kernel, out_shape=list(out_shape), in_specs=[pl.BlockSpec(...  115 us
    all_to_all x5, waiting for transfers between devices, exchange(): lax.all_to_all(shaped, AXES, split_axis=0, concat_axis=0, tiled=True)  49.7 us
    all_to_all x1, blocking collectives, exchange(): lax.all_to_all(shaped, AXES, split_axis=0, concat_axis=0, tiled=True)  41.2 us
    all_to_all x1, blocking collectives, on_device(): lax.all_to_all(outgoing, AXES, split_axis=0, concat_axis=0, tiled=True)  23.5 us
    unnamed x84, local copies, waits for them, and re-layouts  21.1 us
    all_to_all x5, starting transfers between devices, exchange(): lax.all_to_all(shaped, AXES, split_axis=0, concat_axis=0, tiled=True)  18.5 us
    all_to_all x1, starting transfers between devices, on_device(): lax.all_to_all(returning, AXES, split_axis=0, concat_axis=0, tiled=True)  7.37 us
    all_to_all x1, waiting for transfers between devices, on_device(): lax.all_to_all(returning, AXES, split_axis=0, concat_axis=0, tiled=True)  7.23 us
  transfers between devices with their start and end apart: 6, of which 6 were waited for; matrix products, arithmetic and copies ran while one was open for 6% of the time, Pallas kernels for 17%

profile of v2, /device:TPU:0, one launch (start us, length us, event | category | flops | bytes accessed | tf_op | source)
XLA Modules:
  0.0 323.1 jit_solution(7067195857389835807)
XLA Ops:
  0.6 1.1 fusion.25
  1.7 1.1 fusion.24
  2.8 1.0 fusion.27
  3.8 1.0 fusion.26
  4.8 0.9 convert_reduce_fusion.starts_ref
  5.7 0.8 fusion.18
  6.4 6.0 %sort.144 = (s32[4096]{0:T(1024)S(1)}, f32[4096]{0:T(1024)S(1)}, f32[4096]{0:T(1024)S(1)}, f32[4096]{0:T(1024)S(1)}, f32[4096]{0:T(1024)S(1)}, /*index=5*/f32[40...) sort(s32[4096]{0:T(1024)S(1)} %fusion.18, ...), dimensions={0}, to_apply=%region_0.1 | sort | flops 49152 | bytes 524288 | tf_op jit(solution)/shard_map/sort | solution.py:540
  12.4 3.0 expand.1
  15.5 23.5 %all_to_all.40.in_ref = f32[32,16,256]{2,1,0:T(8,128)S(1)} all-to-all(f32[32,16,256]{2,1,0:T(8,128)S(1)} %expand.1), channel_id=1, replica_groups=mesh['row'=4,'col'=8] {'row','col'}, dimensions={0} | all-to-all | bytes 1048576 | tf_op jit(solution)/shard_map/all_to_all | solution.py:546
  38.9 4.8 %groups.1 = (f32[16,8192]{1,0:T(8,128)S(1)}, s32[2,8192]{1,0:T(2,128)S(1)}, s32[2,16]{1,0:T(2,128)S(1)}) custom-call(f32[32,16,256]{2,1,0:T(8,128)S(1)} %all_to_all.40.in_ref), custom_call_target="tpu_custom_call" | custom-call | bytes 1114240 | tf_op jit(solution)/shard_map/groups/pallas_call | solution.py:106
  43.7 1.2 copy-done.9
  45.0 1.0 copy-done.14
  46.0 0.7 copy-done.32
  47.4 16.2 %project.3.refs_7_ = f32[512,512]{1,0:T(8,128)} custom-call(s32[2,16]{1,0:T(2,128)S(1)} %get-tuple-element.43.bound_ref.refs_0_.refs_1_, s32[2,8192]{1,0:T(2,128)S(1)} %get-tuple-element.44.rc_ref.refs_1_.refs_2_, f32[16,8192]{1,0:T(8,128)S(1)} %get-tuple-element.45.pay_ref.refs_2_.refs_3_, bf16[512,512]{1,0:T(8,128)(2,1)S(1)} %copy-done.9, ...), custom_call_target="tpu_custom_call" | custom-call | flops 17179869184 | bytes 2703488 | tf_op jit(solution)/shard_map/project/pallas_call | solution.py:106
  63.6 15.2 %project.4.refs_7_ = f32[512,512]{1,0:T(8,128)S(1)} custom-call(s32[2,16]{1,0:T(2,128)S(1)} %get-tuple-element.43.bound_ref.refs_0_.refs_1_, s32[2,8192]{1,0:T(2,128)S(1)} %get-tuple-element.44.rc_ref.refs_1_.refs_2_, f32[16,8192]{1,0:T(8,128)S(1)} %get-tuple-element.45.pay_ref.refs_2_.refs_3_, bf16[512,512]{1,0:T(8,128)(2,1)S(1)} %copy-done.9, ...), custom_call_target="tpu_custom_call" | custom-call | flops 17179869184 | bytes 2703488 | tf_op jit(solution)/shard_map/project/pallas_call | solution.py:106
  78.9 41.2 %all_to_all.41 = f32[32,16,512]{2,1,0:T(8,128)S(1)} all-to-all(f32[32,16,512]{2,1,0:T(8,128)S(1)} %bitcast.114), channel_id=1, replica_groups=mesh['row'=4,'col'=8] {'row','col'}, dimensions={0} | all-to-all | bytes 2097152 | tf_op jit(solution)/shard_map/all_to_all | solution.py:562
  120.1 2.8 all-to-all-start.1
  123.0 1.0 copy-done.6
  124.0 1.0 copy-done.10
  125.1 1.0 copy-done.15
  126.1 15.2 %project.5 = f32[512,512]{1,0:T(8,128)S(1)} custom-call(s32[2,16]{1,0:T(2,128)S(1)} %get-tuple-element.43.bound_ref.refs_0_.refs_1_, s32[2,8192]{1,0:T(2,128)S(1)} %get-tuple-element.44.rc_ref.refs_1_.refs_2_, f32[16,8192]{1,0:T(8,128)S(1)} %copy-done.6, bf16[512,512]{1,0:T(8,128)(2,1)S(1)} %copy-done.10, bf16[512,512]{1,0:T(8,128)(2,1)S(1)} %copy-done.15, ...), custom_call_target="tpu_custom_call" | custom-call | flops 17179869184 | bytes 2703488 | tf_op jit(solution)/shard_map/project/pallas_call | solution.py:106
  141.3 1.0 copy-done
  142.3 8.0 %all-to-all-done.1 = f32[32,16,512]{2,1,0:T(8,128)S(1)} async-done(((f32[32,16,512]{2,1,0:T(8,128)}), f32[32,16,512]{2,1,0:T(8,128)S(1)}, u32[]{:S(2)}, u32[]{:S(2)}) %all-to-all-start.1) | async-done | bytes 1048608 | tf_op jit(solution)/shard_map/all_to_all | solution.py:562
  150.4 3.2 all-to-all-start.5
  153.6 1.9 broadcast_multiply_fusion
  155.5 2.9 mul.30
  158.5 3.3 %copy.29 = f32[32,2,4,8,64]{4,3,2,1,0:T(8,128)} copy(f32[32,2,4,8,64]{0,4,3,1,2:T(8,128)} %bitcast.130) | data formatting | bytes 1048576 | tf_op jit(solution)/shard_map/mul | solution.py:557
  161.8 2.3 reshape.62.kt_ref.refs_1_
  164.1 1.0 copy-done.2
  165.2 0.9 copy-done.21
  166.1 0.9 copy-done.24
  167.0 0.8 copy-done.29
  167.8 2.3 spectral.3
  170.1 1.0 copy-done.1
  171.1 10.0 %all-to-all-done.5 = f32[32,16,512]{2,1,0:T(8,128)S(1)} async-done(((f32[32,16,512]{2,1,0:T(8,128)}), f32[32,16,512]{2,1,0:T(8,128)S(1)}, u32[]{:S(2)}, u32[]{:S(2)}) %all-to-all-start.5) | async-done | bytes 1048608 | tf_op jit(solution)/shard_map/all_to_all | solution.py:562
  181.1 2.6 all-to-all-start.2
  183.8 1.5 reduce-precision_convert_fusion.1
  185.3 1.0 copy-done.3
  186.3 0.9 copy-done.22
  187.2 0.9 copy-done.25
  188.1 0.8 copy-done.30
  189.0 3.3 %spectral.4 = f32[512,512]{1,0:T(8,128)} custom-call(f32[512,512]{1,0:T(8,128)S(1)} %bitcast.107, f32[256,512]{1,0:T(8,128)S(1)} %copy-done.3, bf16[256,256]{1,0:T(8,128)(2,1)S(1)} %copy-done.19, bf16[256,256]{1,0:T(8,128)(2,1)S(1)} %copy-done.20, bf16[256,256]{1,0:T(8,128)(2,1)S(1)} %copy-done.22, bf16[256,256]{1,0:T(8,128)(2,1)S(1)} %copy-done.25, ...), custom_call_target="tpu_custom_call" | custom-call | flops 1073741824 | bytes 3276800 | tf_op jit(solution)/shard_map/spectral/pallas_call | solution.py:106
  192.3 19.1 %all-to-all-done.2 = f32[32,16,512]{2,1,0:T(8,128)S(1)} async-done(((f32[32,16,512]{2,1,0:T(8,128)}), f32[32,16,512]{2,1,0:T(8,128)S(1)}, u32[]{:S(2)}, u32[]{:S(2)}) %all-to-all-start.2) | async-done | bytes 1048608 | tf_op jit(solution)/shard_map/all_to_all | solution.py:562
  211.4 2.6 all-to-all-start.4
  214.1 3.0 convolution_bitcast_fusion
  217.1 0.8 slice_add_fusion
  218.6 15.9 %sample.3.refs_8_ = f32[2,8192]{1,0:T(2,128)S(1)} custom-call(f32[512,512]{1,0:T(8,128)S(1)} %bitcast.109, s32[2,16]{1,0:T(2,128)S(1)} %get-tuple-element.43.bound_ref.refs_0_.refs_1_, s32[2,8192]{1,0:T(2,128)S(1)} %get-tuple-element.44.rc_ref.refs_1_.refs_2_, f32[16,8192]{1,0:T(8,128)S(1)} %copy-done.7, bf16[512,512]{1,0:T(8,128)(2,1)S(1)} %copy-done.11, ...), custom_call_target="tpu_custom_call" | custom-call | flops 17179869184 | bytes 2769024 | tf_op jit(solution)/shard_map/sample/pallas_call | solution.py:106
  234.6 3.3 %spectral.5 = f32[512,512]{1,0:T(8,128)} custom-call(f32[512,512]{1,0:T(8,128)S(1)} %bitcast.106, f32[256,512]{1,0:T(8,128)S(1)} %copy-done.4, bf16[256,256]{1,0:T(8,128)(2,1)S(1)} %copy-done.19, bf16[256,256]{1,0:T(8,128)(2,1)S(1)} %copy-done.20, bf16[256,256]{1,0:T(8,128)(2,1)S(1)} %copy-done.23, bf16[256,256]{1,0:T(8,128)(2,1)S(1)} %copy-done.26, ...), custom_call_target="tpu_custom_call" | custom-call | flops 1073741824 | bytes 3276800 | tf_op jit(solution)/shard_map/spectral/pallas_call | solution.py:106
  237.9 3.7 %all-to-all-done.4 = f32[32,16,512]{2,1,0:T(8,128)S(1)} async-done(((f32[32,16,512]{2,1,0:T(8,128)}), f32[32,16,512]{2,1,0:T(8,128)S(1)}, u32[]{:S(2)}, u32[]{:S(2)}) %all-to-all-start.4) | async-done | bytes 1048608 | tf_op jit(solution)/shard_map/all_to_all | solution.py:562
  241.6 7.2 %all-to-all-start.6 = ((f32[32,16,512]{2,1,0:T(8,128)}), f32[32,16,512]{2,1,0:T(8,128)S(1)}, u32[]{:S(2)}, u32[]{:S(2)}) async-start(f32[32,16,512]{2,1,0:T(8,128)} %bitcast.41), calls=%async_computation.6 | async-start | bytes 2097152 | tf_op jit(solution)/shard_map/all_to_all | solution.py:562
  249.5 1.0 copy-done.12
  250.5 1.0 copy-done.17
  251.6 15.8 %sample.4.refs_8_ = f32[2,8192]{1,0:T(2,128)S(1)} custom-call(f32[512,512]{1,0:T(8,128)S(1)} %bitcast.108, s32[2,16]{1,0:T(2,128)S(1)} %get-tuple-element.43.bound_ref.refs_0_.refs_1_, s32[2,8192]{1,0:T(2,128)S(1)} %get-tuple-element.44.rc_ref.refs_1_.refs_2_, f32[16,8192]{1,0:T(8,128)S(1)} %copy-done.8, bf16[512,512]{1,0:T(8,128)(2,1)S(1)} %copy-done.12, ...), custom_call_target="tpu_custom_call" | custom-call | flops 17179869184 | bytes 2769024 | tf_op jit(solution)/shard_map/sample/pallas_call | solution.py:106
  267.4 8.9 %all-to-all-done.6 = f32[32,16,512]{2,1,0:T(8,128)S(1)} async-done(((f32[32,16,512]{2,1,0:T(8,128)}), f32[32,16,512]{2,1,0:T(8,128)S(1)}, u32[]{:S(2)}, u32[]{:S(2)}) %all-to-all-start.6) | async-done | bytes 1048608 | tf_op jit(solution)/shard_map/all_to_all | solution.py:562
  276.2 1.0 copy-done.13
  277.3 1.0 copy-done.18
  278.3 15.8 %sample.5 = f32[2,8192]{1,0:T(2,128)S(1)} custom-call(f32[512,512]{1,0:T(8,128)S(1)} %bitcast.111, s32[2,16]{1,0:T(2,128)S(1)} %get-tuple-element.43.bound_ref.refs_0_.refs_1_, s32[2,8192]{1,0:T(2,128)S(1)} %get-tuple-element.44.rc_ref.refs_1_.refs_2_, f32[16,8192]{1,0:T(8,128)S(1)} %copy-done.8, bf16[512,512]{1,0:T(8,128)(2,1)S(1)} %copy-done.13, ...), custom_call_target="tpu_custom_call" | custom-call | flops 17179869184 | bytes 2769024 | tf_op jit(solution)/shard_map/sample/pallas_call | solution.py:106
  294.2 1.3 ungroup.1
  295.5 7.4 %all-to-all-start.7 = ((f32[32,6,256]{2,1,0:T(8,128)}), f32[32,6,256]{2,1,0:T(8,128)S(1)}, u32[]{:S(2)}, u32[]{:S(2)}) async-start(f32[32,6,256]{2,1,0:T(8,128)} %ungroup.1), calls=%async_computation.7 | async-start | bytes 524288 | tf_op jit(solution)/shard_map/all_to_all | solution.py:587
  302.9 3.4 %convolution_bitcast_fusion.2 = f32[6,32,128]{2,0,1:T(8,128)S(1)} fusion(bf16[32,4,128,128]{3,2,1,0:T(8,128)(2,1)} %param.26, bf16[6,32,4,128]{3,1,0,2:T(8,128)(2,1)S(1)} %pad_maximum_fusion.1), kind=kOutput, calls=%fused_computation.2 | convolution fusion | flops 25165824 | bytes 4489216 | tf_op jit(solution)/shard_map/cbnj,bnij->cbi/dot_general | solution.py:504
  306.3 7.2 %all-to-all-done.7.in_ref = f32[32,6,256]{2,1,0:T(8,128)S(1)} async-done(((f32[32,6,256]{2,1,0:T(8,128)}), f32[32,6,256]{2,1,0:T(8,128)S(1)}, u32[]{:S(2)}, u32[]{:S(2)}) %all-to-all-start.7) | async-done | bytes 196640 | tf_op jit(solution)/shard_map/all_to_all | solution.py:587
  313.5 3.1 compact.1
  316.7 5.6 %sort.145 = (s32[4096]{0:T(1024)}, f32[4096]{0:T(1024)S(1)}, f32[4096]{0:T(1024)S(1)}, f32[4096]{0:T(1024)S(1)}, f32[4096]{0:T(1024)S(1)}, /*index=5*/f32[4096]{0:T(1024)S(1)}, f32[4096]{0:T(1024)S(1)}) sort(s32[4096]{0:T(1024)S(1)} %copy-done.40, f32[4096]{0:T(1024)S(1)} %bitcast.137, f32[4096]{0:T(1024)S(1)} %bitcast.136, f32[4096]{0:T(1024)S(1)} %bitcast.135, ...), dimensions={0}, to_apply=%region_2.3 | sort | flops 49152 | bytes 229376 | tf_op jit(solution)/shard_map/sort | solution.py:589
  322.3 0.8 bitcast_add_fusion
  (70 shorter events, 2.3 us)
Async XLA Ops:
  43.7 19.9 %copy-start.5 = (f32[16,8192]{1,0:T(8,128)}, f32[16,8192]{1,0:T(8,128)S(1)}, u32[]{:S(2)}) copy-start(f32[16,8192]{1,0:T(8,128)S(1)} %get-tuple-element.45.pay_ref.refs_2_.refs_3_) | copy-start | bytes 1572868
  43.7 1.2 copy-start.9
  45.0 1.0 copy-start.14
  46.0 0.7 copy-start.32
  46.7 0.7 copy-start.34
  78.9 44.1 %copy-start.33 = (f32[16,128]{1,0:T(8,128)S(1)}, f32[16,128]{1,0:T(8,128)}, u32[]{:S(2)}) copy-start(f32[16,128]{1,0:T(8,128)} %constant.65.clone.cos_ref.refs_5_.refs_6_) | copy-start | bytes 24580
  78.9 44.1 %copy-start.35 = (f32[16,128]{1,0:T(8,128)S(1)}, f32[16,128]{1,0:T(8,128)}, u32[]{:S(2)}) copy-start(f32[16,128]{1,0:T(8,128)} %constant.66.clone.sin_ref.refs_6_.refs_7_) | copy-start | bytes 24580
  120.1 30.2 %all-to-all-start.1 = ((f32[32,16,512]{2,1,0:T(8,128)}), f32[32,16,512]{2,1,0:T(8,128)S(1)}, u32[]{:S(2)}, u32[]{:S(2)}) async-start(f32[32,16,512]{2,1,0:T(8,128)} %bitcast.30), calls=%async_computation.1 | async-start | bytes 2097152 | tf_op jit(solution)/shard_map/all_to_all | solution.py:562
  123.0 1.0 copy-start.6
  124.0 1.0 copy-start.10
  125.1 1.0 copy-start.15
  141.3 1.0 copy-start
  150.4 30.8 %all-to-all-start.5 = ((f32[32,16,512]{2,1,0:T(8,128)}), f32[32,16,512]{2,1,0:T(8,128)S(1)}, u32[]{:S(2)}, u32[]{:S(2)}) async-start(f32[32,16,512]{2,1,0:T(8,128)} %bitcast.112), calls=%async_computation.5 | async-start | bytes 2097152 | tf_op jit(solution)/shard_map/all_to_all | solution.py:562
  153.5 10.6 %copy-start.19 = (bf16[256,256]{1,0:T(8,128)(2,1)S(1)}, bf16[256,256]{1,0:T(8,128)(2,1)}, u32[]{:S(2)}) copy-start(bf16[256,256]{1,0:T(8,128)(2,1)} %constant.69.clone.fh_ref.refs_2_) | copy-start | bytes 393220
  153.6 10.6 %copy-start.20 = (bf16[256,256]{1,0:T(8,128)(2,1)S(1)}, bf16[256,256]{1,0:T(8,128)(2,1)}, u32[]{:S(2)}) copy-start(bf16[256,256]{1,0:T(8,128)(2,1)} %constant.70.clone.fl_ref.refs_3_) | copy-start | bytes 393220
  153.6 10.5 %copy-start.27 = (f32[32,512]{1,0:T(8,128)S(1)}, f32[32,512]{1,0:T(8,128)}, u32[]{:S(2)}) copy-start(f32[32,512]{1,0:T(8,128)} %constant.67.clone.cos_ref.refs_6_) | copy-start | bytes 196612
  164.1 1.0 copy-start.2
  165.2 0.9 copy-start.21
  166.1 0.9 copy-start.24
  167.0 0.8 copy-start.29
  170.1 1.0 copy-start.1
  181.1 30.2 %all-to-all-start.2 = ((f32[32,16,512]{2,1,0:T(8,128)}), f32[32,16,512]{2,1,0:T(8,128)S(1)}, u32[]{:S(2)}, u32[]{:S(2)}) async-start(f32[32,16,512]{2,1,0:T(8,128)} %bitcast.113), calls=%async_computation.2 | async-start | bytes 2097152 | tf_op jit(solution)/shard_map/all_to_all | solution.py:562
  185.3 1.0 copy-start.3
  186.3 0.9 copy-start.22
  187.2 0.9 copy-start.25
  188.1 0.8 copy-start.30
  211.4 30.2 %all-to-all-start.4 = ((f32[32,16,512]{2,1,0:T(8,128)}), f32[32,16,512]{2,1,0:T(8,128)S(1)}, u32[]{:S(2)}, u32[]{:S(2)}) async-start(f32[32,16,512]{2,1,0:T(8,128)} %bitcast.37), calls=%async_computation.4 | async-start | bytes 2097152 | tf_op jit(solution)/shard_map/all_to_all | solution.py:562
  214.0 3.8 %copy-start.7 = (f32[16,8192]{1,0:T(8,128)S(1)}, f32[16,8192]{1,0:T(8,128)}, u32[]{:S(2)}) copy-start(f32[16,8192]{1,0:T(8,128)} %copy-done.5) | copy-start | bytes 1572868
  214.0 3.8 %copy-start.11 = (bf16[512,512]{1,0:T(8,128)(2,1)S(1)}, bf16[512,512]{1,0:T(8,128)(2,1)}, u32[]{:S(2)}) copy-start(bf16[512,512]{1,0:T(8,128)(2,1)} %constant.63.clone.yhi_ref.refs_3_.refs_4_) | copy-start | bytes 1572868
  214.0 3.8 %copy-start.16 = (bf16[512,512]{1,0:T(8,128)(2,1)S(1)}, bf16[512,512]{1,0:T(8,128)(2,1)}, u32[]{:S(2)}) copy-start(bf16[512,512]{1,0:T(8,128)(2,1)} %constant.64.clone.ylo_ref.refs_4_.refs_5_) | copy-start | bytes 1572868
  217.9 0.7 copy-start.36
  218.6 16.0 %copy-start.4 = (f32[256,512]{1,0:T(8,128)S(1)}, f32[256,512]{1,0:T(8,128)}, u32[]{:S(2)}) copy-start(f32[256,512]{1,0:T(8,128)} %reshape.62.kt_ref.refs_1_) | copy-start | bytes 1572868
  218.6 16.0 %copy-start.23 = (bf16[256,256]{1,0:T(8,128)(2,1)S(1)}, bf16[256,256]{1,0:T(8,128)(2,1)}, u32[]{:S(2)}) copy-start(bf16[256,256]{1,0:T(8,128)(2,1)} %constant.71.clone.ih_ref.refs_4_) | copy-start | bytes 393220
  218.6 16.0 %copy-start.26 = (bf16[256,256]{1,0:T(8,128)(2,1)S(1)}, bf16[256,256]{1,0:T(8,128)(2,1)}, u32[]{:S(2)}) copy-start(bf16[256,256]{1,0:T(8,128)(2,1)} %constant.72.clone.il_ref.refs_5_) | copy-start | bytes 393220
  218.6 16.0 %copy-start.28 = (f32[32,512]{1,0:T(8,128)S(1)}, f32[32,512]{1,0:T(8,128)}, u32[]{:S(2)}) copy-start(f32[32,512]{1,0:T(8,128)} %constant.67.clone.cos_ref.refs_6_) | copy-start | bytes 196612
  218.6 16.0 %copy-start.31 = (f32[32,512]{1,0:T(8,128)S(1)}, f32[32,512]{1,0:T(8,128)}, u32[]{:S(2)}) copy-start(f32[32,512]{1,0:T(8,128)} %constant.68.clone.sin_ref.refs_7_) | copy-start | bytes 196612
  234.5 14.4 %copy-start.38 = (f32[3,32,4,128]{3,0,2,1:T(4,128)S(1)}, f32[3,32,4,128]{3,0,2,1:T(4,128)}, u32[]{:S(2)}) copy-start(f32[3,32,4,128]{3,0,2,1:T(4,128)} %slice_add_fusion) | copy-start | bytes 589828
  234.5 14.4 %copy-start.41 = (s32[32,4]{0,1:T(4,128)S(1)}, s32[32,4]{0,1:T(4,128)}, u32[]{:S(2)}) copy-start(s32[32,4]{0,1:T(4,128)} %param.25) | copy-start | bytes 1540
  234.5 14.7 %copy-start.39 = (f32[3,4096]{1,0:T(4,128)S(1)}, f32[3,4096]{1,0:T(4,128)}, u32[]{:S(2)}) copy-start(f32[3,4096]{1,0:T(4,128)} %param.19) | copy-start | bytes 147460
  234.5 15.0 %copy-start.8 = (f32[16,8192]{1,0:T(8,128)S(1)}, f32[16,8192]{1,0:T(8,128)}, u32[]{:S(2)}) copy-start(f32[16,8192]{1,0:T(8,128)} %copy-done.5) | copy-start | bytes 1572868
  234.5 15.0 %copy-start.37 = (f32[16,128]{1,0:T(8,128)S(1)}, f32[16,128]{1,0:T(8,128)}, u32[]{:S(2)}) copy-start(f32[16,128]{1,0:T(8,128)} %constant.66.clone.sin_ref.refs_6_.refs_7_) | copy-start | bytes 24580
  241.6 34.6 %all-to-all-start.6 = ((f32[32,16,512]{2,1,0:T(8,128)}), f32[32,16,512]{2,1,0:T(8,128)S(1)}, u32[]{:S(2)}, u32[]{:S(2)}) async-start(f32[32,16,512]{2,1,0:T(8,128)} %bitcast.41), calls=%async_computation.6 | async-start | bytes 2097152 | tf_op jit(solution)/shard_map/all_to_all | solution.py:562
  249.5 1.0 copy-start.12
  250.5 1.0 copy-start.17
  276.2 1.0 copy-start.13
  277.3 1.0 copy-start.18
  294.1 22.6 %copy-start.40 = (s32[4096]{0:T(1024)S(1)}, s32[4096]{0:T(1024)}, u32[]{:S(2)}) copy-start(s32[4096]{0:T(1024)} %get-tuple-element.27) | copy-start | bytes 49156
  295.5 18.0 %all-to-all-start.7 = ((f32[32,6,256]{2,1,0:T(8,128)}), f32[32,6,256]{2,1,0:T(8,128)S(1)}, u32[]{:S(2)}, u32[]{:S(2)}) async-start(f32[32,6,256]{2,1,0:T(8,128)} %ungroup.1), calls=%async_computation.7 | async-start | bytes 524288 | tf_op jit(solution)/shard_map/all_to_all | solution.py:587
